TPU v7x, 32 devices: a whole 2x2x4 slice. The times are simulated.
32 devices in a mesh: dp: 16 (over z, x, core), seq: 2 (over y).
Axes of the slice: x: 2, y: 2, z: 4, core: 2. Of those that a mesh axis runs over, the one named last changes fastest.
Arguments:
- images: bfloat16 [32, 592, 1024], P('dp', 'seq'), may hold values from -6 to 6
- cotangent: bfloat16 [32, 592, 1024], P('dp', 'seq'), may hold values from -6 to 6
- w_qkv: float32 [1024, 3072], P('dp', 'seq'), may hold values from -0.1875 to 0.1875
- w_out: float32 [1024, 1024], P('dp', 'seq'), may hold values from -1 to 1
- w_up: float32 [1024, 4096], P('dp', 'seq'), may hold values from -0.1875 to 0.1875
- w_down: float32 [4096, 1024], P('dp', 'seq'), may hold values from -0.09375 to 0.09375
- gains: float32 [2, 1024], P(None, ('dp', 'seq')), may hold values from 0.5 to 1.5
- biases: float32 [10, 1024], P(None, ('dp', 'seq')), may hold values from -3 to 3
- first_qkv: float32 [1024, 3072], P('dp', 'seq'), may hold values from -120 to 120
- first_out: float32 [1024, 1024], P('dp', 'seq'), may hold values from -120 to 120
- first_up: float32 [1024, 4096], P('dp', 'seq'), may hold values from -120 to 120
- first_down: float32 [4096, 1024], P('dp', 'seq'), may hold values from -120 to 120
- first_gains: float32 [2, 1024], P(None, ('dp', 'seq')), may hold values from -120 to 120
- first_biases: float32 [10, 1024], P(None, ('dp', 'seq')), may hold values from -120 to 120
- second_qkv: float32 [1024, 3072], P('dp', 'seq'), may hold values from 100 to 10000
- second_out: float32 [1024, 1024], P('dp', 'seq'), may hold values from 100 to 10000
- second_up: float32 [1024, 4096], P('dp', 'seq'), may hold values from 100 to 10000
- second_down: float32 [4096, 1024], P('dp', 'seq'), may hold values from 100 to 10000
- second_gains: float32 [2, 1024], P(None, ('dp', 'seq')), may hold values from 100 to 10000
- second_biases: float32 [10, 1024], P(None, ('dp', 'seq')), may hold values from 100 to 10000
Outputs:
- out_images: bfloat16 [32, 592, 1024], P('dp', 'seq')
- grad_images: bfloat16 [32, 592, 1024], P('dp', 'seq')
- grad_qkv: float32 [1024, 3072], P('dp', 'seq')
- grad_out: float32 [1024, 1024], P('dp', 'seq')
- grad_up: float32 [1024, 4096], P('dp', 'seq')
- grad_down: float32 [4096, 1024], P('dp', 'seq')
- grad_gains: float32 [2, 1024], P(None, ('dp', 'seq'))
- grad_biases: float32 [10, 1024], P(None, ('dp', 'seq'))
- new_qkv: float32 [1024, 3072], P('dp', 'seq')
- new_out: float32 [1024, 1024], P('dp', 'seq')
- new_up: float32 [1024, 4096], P('dp', 'seq')
- new_down: float32 [4096, 1024], P('dp', 'seq')
- new_gains: float32 [2, 1024], P(None, ('dp', 'seq'))
- new_biases: float32 [10, 1024], P(None, ('dp', 'seq'))
- new_first_qkv: float32 [1024, 3072], P('dp', 'seq')
- new_first_out: float32 [1024, 1024], P('dp', 'seq')
- new_first_up: float32 [1024, 4096], P('dp', 'seq')
- new_first_down: float32 [4096, 1024], P('dp', 'seq')
- new_first_gains: float32 [2, 1024], P(None, ('dp', 'seq'))
- new_first_biases: float32 [10, 1024], P(None, ('dp', 'seq'))
- new_second_qkv: float32 [1024, 3072], P('dp', 'seq')
- new_second_out: float32 [1024, 1024], P('dp', 'seq')
- new_second_up: float32 [1024, 4096], P('dp', 'seq')
- new_second_down: float32 [4096, 1024], P('dp', 'seq')
- new_second_gains: float32 [2, 1024], P(None, ('dp', 'seq'))
- new_second_biases: float32 [10, 1024], P(None, ('dp', 'seq'))
All inputs are finite; a program needn't handle non-finite values.
Results may differ from a plain program's by a relative error of at most 0.028.
Values may be sent and summed in bfloat16 or wider, within the bound.
A program may use at most 256 MiB of HBM per device.

v0:
```python
import jax
import jax.numpy as jnp
from jax import lax
from jax.experimental import pallas as pl
from jax.experimental.pallas import tpu as pltpu
from jax.sharding import PartitionSpec as P

HEAD_DIM = 64
PATCH_TOK = 577
STEP = 5


def normalize(rows):
    center = rows - jnp.mean(rows, axis=-1, keepdims=True)
    inverse = lax.rsqrt(jnp.mean(center * center, axis=-1, keepdims=True) + 1e-06)
    return (center * inverse, inverse)


def norm_back(grad_out, normed, inverse, gain):
    scaled = grad_out * gain
    return inverse * (
        scaled
        - jnp.mean(scaled, axis=-1, keepdims=True)
        - normed * jnp.mean(scaled * normed, axis=-1, keepdims=True)
    )


def gelu_value(pre):
    return pre * 0.5 * (1.0 + lax.erf(pre * 0.7071067811865476))


def gelu_slope(pre):
    return (
        0.5 * (1.0 + lax.erf(pre * 0.7071067811865476))
        + pre * jnp.exp(-0.5 * pre * pre) * 0.3989422804014327
    )


def adamw(param, grad, first, second):
    first_new = 0.9 * first + 0.1 * grad
    second_new = 0.95 * second + 0.05 * grad * grad
    step_size = first_new / (1.0 - 0.9**STEP) / (jnp.sqrt(second_new / (1.0 - 0.95**STEP)) + 1e-08)
    return (param - 0.004 * (step_size + 0.05 * param), first_new, second_new)


LANES = 128
NT = (((1,), (1,)), ((), ()))
NN = (((1,), (0,)), ((), ()))
TN = (((0,), (0,)), ((), ()))


def dot(a, b, dims):
    return lax.dot_general(a, b, dims, preferred_element_type=jnp.float32)


def head_masks(rows, dtype):
    lane = lax.broadcasted_iota(jnp.int32, (rows, LANES), 1)
    return [
        ((lane >= h * HEAD_DIM) & (lane < (h + 1) * HEAD_DIM)) for h in range(LANES // HEAD_DIM)
    ]


def attend_kernel(q_ref, k_ref, v_ref, live_ref, ctx_ref):
    q, k, v = q_ref[0], k_ref[0], v_ref[0]
    live = live_ref[...] > 0.5
    total = jnp.zeros(q.shape, jnp.float32)
    zero = jnp.zeros_like(q)
    for mask in head_masks(q.shape[0], q.dtype):
        scores = dot(jnp.where(mask, q, zero), k, NT) * (HEAD_DIM**-0.5)
        scores = jnp.where(live, scores, -1e30)
        top = jnp.max(scores, axis=-1, keepdims=True)
        weights = jnp.exp(scores - top)
        denom = jnp.sum(weights, axis=-1, keepdims=True)
        probs = (weights * (1.0 / denom)).astype(jnp.bfloat16)
        total = jnp.where(mask, dot(probs, v, NN), total)
    ctx_ref[0] = total.astype(jnp.bfloat16)


def attend_back_kernel(q_ref, k_ref, v_ref, g_ref, live_ref, dq_ref, dk_ref, dv_ref):
    q, k, v, g = q_ref[0], k_ref[0], v_ref[0], g_ref[0]
    live = live_ref[...] > 0.5
    zero_q = jnp.zeros_like(q)
    zero_k = jnp.zeros_like(k)
    dq = jnp.zeros(q.shape, jnp.float32)
    dk = jnp.zeros(k.shape, jnp.float32)
    dv = jnp.zeros(k.shape, jnp.float32)
    masks_q = head_masks(q.shape[0], q.dtype)
    masks_k = head_masks(k.shape[0], k.dtype)
    for mask, mask_k in zip(masks_q, masks_k):
        q_h = jnp.where(mask, q, zero_q)
        g_h = jnp.where(mask, g, zero_q)
        k_h = jnp.where(mask_k, k, zero_k)
        scores = dot(k, q_h, NT) * (HEAD_DIM**-0.5)
        scores = jnp.where(live, scores, -1e30)
        top = jnp.max(scores, axis=0, keepdims=True)
        weights = jnp.exp(scores - top)
        denom = jnp.sum(weights, axis=0, keepdims=True)
        probs = weights * (1.0 / denom)
        grad_probs = dot(v, g_h, NT)
        delta = jnp.sum(probs * grad_probs, axis=0, keepdims=True)
        grad_scores = (probs * (grad_probs - delta) * (HEAD_DIM**-0.5)).astype(jnp.bfloat16)
        dv = dv + dot(probs.astype(jnp.bfloat16), g_h, NN)
        dk = dk + dot(grad_scores, q_h, NN)
        dq = dq + dot(grad_scores, k_h, TN)
    dq_ref[0] = dq
    dk_ref[0] = dk.astype(dk_ref.dtype)
    dv_ref[0] = dv.astype(dv_ref.dtype)


def attend(queries, keys, values, live):
    count, rows, width = queries.shape
    length = keys.shape[1]
    q_spec = pl.BlockSpec((1, rows, LANES), lambda i, h: (i, 0, h))
    k_spec = pl.BlockSpec((1, length, LANES), lambda i, h: (i, 0, h))
    pairs = count * rows * length * width
    return pl.pallas_call(
        attend_kernel,
        grid=(count, width // LANES),
        in_specs=[q_spec, k_spec, k_spec, pl.BlockSpec((1, length), lambda i, h: (0, 0))],
        out_specs=q_spec,
        out_shape=jax.ShapeDtypeStruct(queries.shape, jnp.bfloat16),
        cost_estimate=pl.CostEstimate(
            flops=8 * pairs, bytes_accessed=8 * queries.size, transcendentals=pairs // HEAD_DIM
        ),
        compiler_params=pltpu.CompilerParams(vmem_limit_bytes=48 * 1024 * 1024),
    )(queries, keys, values, live.reshape(1, length))


def attend_back(queries, keys, values, grad_ctx, live, back_dtype):
    count, rows, width = queries.shape
    length = keys.shape[1]
    q_spec = pl.BlockSpec((1, rows, LANES), lambda i, h: (i, 0, h))
    k_spec = pl.BlockSpec((1, length, LANES), lambda i, h: (i, 0, h))
    pairs = count * rows * length * width
    return pl.pallas_call(
        attend_back_kernel,
        grid=(count, width // LANES),
        in_specs=[q_spec, k_spec, k_spec, q_spec, pl.BlockSpec((length, 1), lambda i, h: (0, 0))],
        out_specs=[q_spec, k_spec, k_spec],
        out_shape=[
            jax.ShapeDtypeStruct(queries.shape, jnp.float32),
            jax.ShapeDtypeStruct(keys.shape, back_dtype),
            jax.ShapeDtypeStruct(keys.shape, back_dtype),
        ],
        cost_estimate=pl.CostEstimate(
            flops=20 * pairs, bytes_accessed=20 * queries.size, transcendentals=pairs // HEAD_DIM
        ),
        compiler_params=pltpu.CompilerParams(vmem_limit_bytes=56 * 1024 * 1024),
    )(queries, keys, values, grad_ctx, live.reshape(length, 1))


def shift_by(step, ways):
    return [(i, (i + step) % ways) for i in range(ways)]


def spread(tokens):
    ways = lax.axis_size("seq")
    me = lax.axis_index("seq")
    each = tokens.shape[0] // ways
    parts = [lax.dynamic_slice_in_dim(tokens, me * each, each, 0)]
    for step in range(1, ways):
        target = lax.rem(me + step, ways)
        piece = lax.dynamic_slice_in_dim(tokens, target * each, each, 0)
        parts.append(lax.ppermute(piece, "seq", shift_by(step, ways)))
    return jnp.concatenate(parts, axis=1)


def unspread(tokens):
    ways = lax.axis_size("seq")
    me = lax.axis_index("seq")
    each, length, width = tokens.shape
    group = length // ways
    result = jnp.zeros((each * ways, group, width), tokens.dtype)
    for step in range(ways):
        piece = tokens[:, step * group : (step + 1) * group]
        if step:
            piece = lax.ppermute(piece, "seq", shift_by(-step, ways))
        source = lax.rem(me + step, ways)
        result = lax.dynamic_update_slice_in_dim(result, piece, source * each, 0)
    return result


def sum_over_seq(terms, axis):
    ways = lax.axis_size("seq")
    me = lax.axis_index("seq")
    size = terms.shape[axis] // ways
    total = lax.dynamic_slice_in_dim(terms, me * size, size, axis).astype(jnp.float32)
    for step in range(1, ways):
        target = lax.rem(me + step, ways)
        piece = lax.dynamic_slice_in_dim(terms, target * size, size, axis)
        total = total + lax.ppermute(piece, "seq", shift_by(step, ways)).astype(jnp.float32)
    return total


def body(
    images,
    cotangent,
    w_qkv,
    w_out,
    w_up,
    w_down,
    gains,
    biases,
    first_qkv,
    first_out,
    first_up,
    first_down,
    first_gains,
    first_biases,
    second_qkv,
    second_out,
    second_up,
    second_down,
    second_gains,
    second_biases,
):
    params = (w_qkv, w_out, w_up, w_down, gains, biases)
    firsts = (first_qkv, first_out, first_up, first_down, first_gains, first_biases)
    seconds = (second_qkv, second_out, second_up, second_down, second_gains, second_biases)
    count, group, width = images.shape
    ways = lax.axis_size("seq")
    blocks = lax.axis_size("dp")
    me = lax.axis_index("seq")
    pad_len = group * ways
    by_image = count % ways == 0
    rows_dp = w_qkv.shape[0]
    cols = w_out.shape[1]
    fold = w_up.shape[1] // cols
    own = gains.shape[1]
    small = jnp.concatenate([gains, biases], axis=0).astype(jnp.bfloat16).T
    lanes = -(-small.shape[1] // LANES) * LANES
    small = jnp.pad(small, ((0, rows_dp - own), (0, lanes - small.shape[1])))
    part_a = jnp.concatenate([w_qkv.astype(jnp.bfloat16), small], axis=1)
    wide_a = lax.all_gather(part_a, ("seq", "dp"), axis=0, tiled=True)
    part_b = jnp.concatenate(
        [
            w_out.astype(jnp.bfloat16),
            w_up.astype(jnp.bfloat16)
            .reshape(rows_dp, fold, cols)
            .transpose(1, 0, 2)
            .reshape(fold * rows_dp, cols),
            w_down.astype(jnp.bfloat16),
        ],
        axis=0,
    )
    part_b, wide_a = lax.optimization_barrier((part_b, wide_a))
    wide_b = lax.all_gather(part_b, ("seq", "dp"), axis=0, tiled=True)
    wide_a = wide_a.reshape(ways, width, part_a.shape[1])
    wide_qkv = jnp.concatenate([wide_a[k, :, : w_qkv.shape[1]] for k in range(ways)], axis=1)
    wide_small = (
        wide_a.reshape(ways, blocks, rows_dp, part_a.shape[1])[
            :, :, :own, w_qkv.shape[1] : w_qkv.shape[1] + 12
        ]
        .astype(jnp.float32)
        .transpose(3, 1, 0, 2)
        .reshape(12, width)
    )
    gain, bias = wide_small[:2], wide_small[2:]
    back_gain = gain
    wide_b = wide_b.reshape(ways, blocks, part_b.shape[0], cols)
    wide_out = wide_b[:, :, :rows_dp].transpose(1, 2, 0, 3).reshape(width, width)
    wide_up = (
        wide_b[:, :, rows_dp : (1 + fold) * rows_dp]
        .reshape(ways, blocks, fold, rows_dp, cols)
        .transpose(1, 3, 0, 2, 4)
        .reshape(width, fold * width)
    )
    wide_down = (
        wide_b[:, :, (1 + fold) * rows_dp :].transpose(1, 2, 0, 3).reshape(fold * width, width)
    )
    back_qkv, back_out, back_up, back_down = wide_qkv, wide_out, wide_up, wide_down
    spot = jnp.arange(group, dtype=jnp.int32)
    if by_image:
        images, cotangent = spread(images), spread(cotangent)
        token_live = jnp.concatenate(
            [lax.rem(me - k + ways, ways) * group + spot for k in range(ways)]
        ) < PATCH_TOK
        key_live = token_live
    else:
        token_live = me * group + spot < PATCH_TOK
        key_live = jnp.arange(pad_len, dtype=jnp.int32) < PATCH_TOK
    query_live = token_live
    key_live = key_live.astype(jnp.float32)
    rows = images.astype(jnp.float32)
    normed_a, inverse_a = normalize(rows)
    hidden_a = (normed_a * gain[0] + bias[0]).astype(jnp.bfloat16)
    mixed = jnp.einsum("icd,de->ice", hidden_a, wide_qkv, preferred_element_type=jnp.float32)
    queries = (mixed[..., :width] + bias[1]).astype(jnp.bfloat16)
    keys = mixed[..., width : 2 * width].astype(jnp.bfloat16)
    values = (mixed[..., 2 * width :] + bias[2]).astype(jnp.bfloat16)
    if by_image:
        keys_all, values_all = keys, values
    else:
        keys_all, values_all = (
            lax.all_gather(keys, "seq", axis=1, tiled=True),
            lax.all_gather(values, "seq", axis=1, tiled=True),
        )
    context = attend(queries, keys_all, values_all, key_live)
    resid = (
        rows
        + jnp.einsum("icd,de->ice", context, wide_out, preferred_element_type=jnp.float32)
        + bias[3]
    )
    normed_b, inverse_b = normalize(resid)
    hidden_b = (normed_b * gain[1] + bias[4]).astype(jnp.bfloat16)
    pre = jnp.einsum("icd,df->icf", hidden_b, wide_up, preferred_element_type=jnp.float32) + bias[
        6:
    ].reshape(-1)
    active = gelu_value(pre).astype(jnp.bfloat16)
    out_images = (
        resid
        + jnp.einsum("icf,fd->icd", active, wide_down, preferred_element_type=jnp.float32)
        + bias[5]
    ).astype(jnp.bfloat16)
    grad_y = cotangent.astype(jnp.float32) * query_live[None, :, None].astype(jnp.float32)
    grad_yb = grad_y.astype(jnp.bfloat16)
    g_down = jnp.einsum("icf,icd->fd", active, grad_yb, preferred_element_type=jnp.float32)
    grad_pre = jnp.einsum(
        "icd,fd->icf", grad_yb, back_down, preferred_element_type=jnp.float32
    ) * gelu_slope(pre)
    grad_preb = grad_pre.astype(jnp.bfloat16)
    g_up = jnp.einsum("icd,icf->df", hidden_b, grad_preb, preferred_element_type=jnp.float32)
    grad_hb = jnp.einsum("icf,df->icd", grad_preb, back_up, preferred_element_type=jnp.float32)
    grad_resid = grad_y + norm_back(grad_hb, normed_b, inverse_b, back_gain[1])
    grad_rb = grad_resid.astype(jnp.bfloat16)
    g_outw = jnp.einsum("icd,ice->de", context, grad_rb, preferred_element_type=jnp.float32)
    grad_ctx = jnp.einsum(
        "ice,de->icd", grad_rb, back_out, preferred_element_type=jnp.float32
    ).astype(jnp.bfloat16)
    grad_q, grad_k, grad_v = attend_back(
        queries,
        keys_all,
        values_all,
        grad_ctx,
        key_live,
        jnp.float32 if by_image else jnp.bfloat16,
    )
    if not by_image:
        grad_k, grad_v = (
            lax.psum_scatter(grad_k, "seq", scatter_dimension=1, tiled=True).astype(jnp.float32),
            lax.psum_scatter(grad_v, "seq", scatter_dimension=1, tiled=True).astype(jnp.float32),
        )
    grad_mixed = jnp.concatenate([grad_q, grad_k, grad_v], axis=-1).astype(jnp.bfloat16)
    g_qkv = jnp.einsum("icd,ice->de", hidden_a, grad_mixed, preferred_element_type=jnp.float32)
    grad_ha = jnp.einsum("ice,de->icd", grad_mixed, back_qkv, preferred_element_type=jnp.float32)
    grad_images = (grad_resid + norm_back(grad_ha, normed_a, inverse_a, back_gain[0])).astype(
        jnp.bfloat16
    )
    g_gains = jnp.stack(
        [jnp.sum(grad_ha * normed_a, axis=(0, 1)), jnp.sum(grad_hb * normed_b, axis=(0, 1))]
    )
    g_biases = jnp.concatenate(
        [
            jnp.stack(
                [
                    jnp.sum(grad_ha, axis=(0, 1)),
                    jnp.sum(grad_q, axis=(0, 1)),
                    jnp.sum(grad_v, axis=(0, 1)),
                    jnp.sum(grad_resid, axis=(0, 1)),
                    jnp.sum(grad_hb, axis=(0, 1)),
                    jnp.sum(grad_y, axis=(0, 1)),
                ]
            ),
            jnp.sum(grad_pre, axis=(0, 1)).reshape(-1, width),
        ],
        axis=0,
    )
    if by_image:
        out_images, grad_images = unspread(out_images), unspread(grad_images)
    send_a = jnp.concatenate(
        [
            g_outw.astype(jnp.bfloat16).reshape(blocks, rows_dp, width),
            g_up.astype(jnp.bfloat16)
            .reshape(blocks, rows_dp, ways, fold, cols)
            .transpose(0, 3, 1, 2, 4)
            .reshape(blocks, fold * rows_dp, width),
            g_down.astype(jnp.bfloat16).reshape(blocks, fold * rows_dp, width),
        ],
        axis=1,
    ).reshape(-1, width)
    part = lax.psum_scatter(send_a, "dp", scatter_dimension=0, tiled=True)
    total_a = sum_over_seq(part, 1)
    g_small = jnp.concatenate([g_gains, g_biases], axis=0).astype(jnp.bfloat16).T
    g_small = jnp.pad(g_small, ((0, 0), (0, lanes - g_small.shape[1])))
    send_b = jnp.concatenate([g_qkv.astype(jnp.bfloat16), g_small], axis=1)
    part, _ = lax.optimization_barrier((send_b, part))
    part = lax.psum_scatter(part, "dp", scatter_dimension=0, tiled=True)
    total_qkv = sum_over_seq(part[:, : g_qkv.shape[1]], 1)
    total_small = sum_over_seq(part[:, g_qkv.shape[1] :], 0)[:, :12].T
    totals = (
        total_qkv,
        total_a[:rows_dp],
        total_a[rows_dp : (1 + fold) * rows_dp]
        .reshape(fold, rows_dp, cols)
        .transpose(1, 0, 2)
        .reshape(rows_dp, fold * cols),
        total_a[(1 + fold) * rows_dp :],
        total_small[:2],
        total_small[2:],
    )
    updated = [
        adamw(param, grad, first, second)
        for param, grad, first, second in zip(params, totals, firsts, seconds)
    ]
    news = tuple((entry[0] for entry in updated))
    new_firsts = tuple((entry[1] for entry in updated))
    new_seconds = tuple((entry[2] for entry in updated))
    return (
        out_images,
        grad_images,
        totals[0],
        totals[1],
        totals[2],
        totals[3],
        totals[4],
        totals[5],
        news[0],
        news[1],
        news[2],
        news[3],
        news[4],
        news[5],
        new_firsts[0],
        new_firsts[1],
        new_firsts[2],
        new_firsts[3],
        new_firsts[4],
        new_firsts[5],
        new_seconds[0],
        new_seconds[1],
        new_seconds[2],
        new_seconds[3],
        new_seconds[4],
        new_seconds[5],
    )


def solution(mesh):
    return jax.shard_map(
        body,
        mesh=mesh,
        in_specs=(
            P("dp", "seq", None),
            P("dp", "seq", None),
            P("dp", "seq"),
            P("dp", "seq"),
            P("dp", "seq"),
            P("dp", "seq"),
            P(None, ("dp", "seq")),
            P(None, ("dp", "seq")),
            P("dp", "seq"),
            P("dp", "seq"),
            P("dp", "seq"),
            P("dp", "seq"),
            P(None, ("dp", "seq")),
            P(None, ("dp", "seq")),
            P("dp", "seq"),
            P("dp", "seq"),
            P("dp", "seq"),
            P("dp", "seq"),
            P(None, ("dp", "seq")),
            P(None, ("dp", "seq")),
        ),
        out_specs=(
            P("dp", "seq", None),
            P("dp", "seq", None),
            P("dp", "seq"),
            P("dp", "seq"),
            P("dp", "seq"),
            P("dp", "seq"),
            P(None, ("dp", "seq")),
            P(None, ("dp", "seq")),
            P("dp", "seq"),
            P("dp", "seq"),
            P("dp", "seq"),
            P("dp", "seq"),
            P(None, ("dp", "seq")),
            P(None, ("dp", "seq")),
            P("dp", "seq"),
            P("dp", "seq"),
            P("dp", "seq"),
            P("dp", "seq"),
            P(None, ("dp", "seq")),
            P(None, ("dp", "seq")),
            P("dp", "seq"),
            P("dp", "seq"),
            P("dp", "seq"),
            P("dp", "seq"),
            P(None, ("dp", "seq")),
            P(None, ("dp", "seq")),
        ),
        check_vma=False,
    )
```

profile of v0, /device:TPU:0, one launch (start us, length us, event | category | flops | bytes accessed | tf_op | source)
XLA Modules:
  0.0 709.9 jit_solution(6612714012748631889)
XLA Ops:
  10.6 1.1 convert_element_type.209
  11.7 1.1 convert_element_type.208
  13.7 71.5 %all-gather.3.cloned.1.call-done = bf16[2048,1664]{1,0:T(8,128)(2,1)} async-done(((bf16[64,1664]{1,0:T(8,128)(2,1)}), bf16[2048,1664]{1,0:T(8,128)(2,1)}) %all-gather.3.cloned.1.call-update) | async-done | bytes 6815760 | tf_op jit(solution)/shard_map/all_gather | solution.py:234
  86.2 1.5 collective-permute-start
  87.6 1.2 constant_dynamic-slice_fusion.6
  89.5 17.6 %collective-permute-done = bf16[1,296,1024]{2,1,0:T(8,128)(2,1)S(1)} collective-permute-done((bf16[1,296,1024]{2,1,0:T(8,128)(2,1)}, bf16[1,296,1024]{2,1,0:T(8,128)(2,1)S(1)}, u32[]{:S(2)}, u32[]{:S(2)}) %collective-permute-start) | collective-permute-done | bytes 606240 | tf_op jit(solution)/shard_map/ppermute | solution.py:164
  110.3 3.3 slice_bitcast_fusion.2
  113.6 4.1 convolution_bitcast_fusion
  117.8 3.0 copy-done.15
  121.2 3.2 fusion.24
  124.5 17.3 %shard_map.395 = bf16[1,592,1024]{2,1,0:T(8,128)(2,1)S(1)} custom-call(bf16[1,592,1024]{2,1,0:T(8,128)(2,1)S(1)} %get-tuple-element.229.q_ref, bf16[1,592,1024]{2,1,0:T(8,128)(2,1)S(1)} %slice.191.k_ref, bf16[1,592,1024]{2,1,0:T(8,128)(2,1)S(1)} %get-tuple-element.228.v_ref, f32[1,592]{1,0:T(1,128)S(1)} %compare_convert_fusion.1.live_ref), custom_call_target="tpu_custom_call" | custom-call | flops 2871001088 | bytes 4849664 | tf_op jit(solution)/shard_map/pallas_call | solution.py:116
  142.8 1.0 copy-done.3
  143.8 69.8 %all-gather.5.cloned.1.call-done = bf16[18432,512]{1,0:T(8,128)(2,1)} async-done(((bf16[576,512]{1,0:T(8,128)(2,1)}), bf16[18432,512]{1,0:T(8,128)(2,1)}) %all-gather.5.cloned.1.call-update) | async-done | bytes 18874384 | tf_op jit(solution)/shard_map/all_gather | solution.py:247
  213.6 1.8 slice_bitcast_fusion.3
  215.5 9.3 %slice_bitcast_fusion = (bf16[16,256,2,512]{3,1,0,2:T(8,128)(2,1)}, bf16[2,16,256,512]{3,2,1,0:T(8,128)(2,1)S(1)}) fusion(bf16[2,16,576,512]{3,2,1,0:T(8,128)(2,1)} %bitcast.97), kind=kLoop, calls=%fused_computation.11 | loop fusion | bytes 33554432 | tf_op jit(solution)/shard_map/transpose | solution.py:269
  224.8 2.2 copy.206
  226.9 2.0 copy.235
  228.9 7.5 %copy.207 = bf16[16,64,2,4,512]{4,3,2,1,0:T(4,128)(2,1)} copy(bf16[16,64,2,4,512]{4,1,3,0,2:T(8,128)(2,1)S(1)} %bitcast.95) | data formatting | bytes 16777216 | tf_op jit(solution)/shard_map/transpose | solution.py:265
  236.4 14.5 %reshape.703 = bf16[1024,4096]{1,0:T(8,128)(2,1)} reshape(bf16[16,64,2,4,512]{4,3,2,1,0:T(4,128)(2,1)} %copy.207) | data formatting | bytes 16777216 | tf_op jit(solution)/shard_map/reshape | solution.py:266
  250.9 3.3 fusion.74
  255.0 11.0 %multiply_convert_fusion = (bf16[592,4096]{1,0:T(8,128)(2,1)}, f32[592,4096]{1,0:T(8,128)}) fusion(f32[4096]{0:T(1024)S(1)} %add.337, bf16[1024,4096]{1,0:T(8,128)(2,1)S(1)} %bitcast.106, f32[592,1024]{1,0:T(8,128)S(1)} %get-tuple-element.259, f32[1024]{0:T(1024)S(1)} %add.334, f32[1024]{0:T(1024)S(1)} %mul.440, f32[592]{0:T(1024)S(1)} %add_rsqrt_fusion, ...), kind=kOutput, calls=%fused_computation.9 | convolution fusion | flops 4983635968 | bytes 25391744 | tf_op jit(solution)/shard_map/icd,df->icf/dot_general | solution.py:306
  266.0 15.0 %copy.208 = bf16[16,256,2,512]{1,0,3,2:T(8,128)(2,1)} copy(bf16[16,256,2,512]{3,1,0,2:T(8,128)(2,1)} %get-tuple-element.226) | data formatting | bytes 16777216 | tf_op jit(solution)/shard_map/transpose | solution.py:269
  281.0 12.4 %copy.236 = bf16[128,8,16,256]{3,1,2,0:T(8,128)(2,1)} copy(bf16[128,8,16,256]{3,2,1,0:T(8,128)(2,1)} %bitcast.91) | data formatting | bytes 16777216
  293.4 12.3 %fusion.75 = (bf16[4096]{0:T(1024)(128)(2,1)S(1)}, bf16[592,4096]{1,0:T(8,128)(2,1)S(1)}) fusion(f32[592,4096]{1,0:T(8,128)} %get-tuple-element.261, f32[4096]{0:T(1024)S(1)} %add.337, bf16[4096,1024]{0,1:T(8,128)(2,1)} %bitcast.103, bf16[1,296,1,1,1,1,1024]{6,1,5,4,3,2,0:T(8,128)(2,1)} %bitcast.21, ...), kind=kOutput, calls=%fused_computation.160 | convolution fusion | flops 4998787072 | bytes 24176960 | tf_op jit(solution)/shard_map/icd,fd->icf/dot_general | solution.py:318
  305.7 9.7 %multiply_reduce_fusion.1 = (bf16[1024]{0:T(1024)(128)(2,1)S(1)}, f32[592]{0:T(1024)S(1)}, f32[592]{0:T(1024)S(1)}, bf16[1024]{0:T(1024)(128)(2,1)S(1)}, f32[592,1024]{1,0:T(8,128)}) fusion(f32[592,1024]{1,0:T(8,128)S(1)} %copy-done.8, f32[592]{0:T(1024)S(1)} %add_rsqrt_fusion, f32[592]{0:T(1024)S(1)} %broadcast_multiply_fusion.4, f32[1024]{0:T(1024)S(1)} %mul.440, ...), kind=kOutput, calls=%fused_computation.49 | convolution fusion | flops 4971508736 | bytes 18105600 | tf_op jit(solution)/shard_map/icf,df->icd/dot_general | solution.py:323
  315.4 9.6 %convolution_convert_fusion = bf16[1024,4096]{1,0:T(8,128)(2,1)} fusion(bf16[592,4096]{1,0:T(8,128)(2,1)S(1)} %get-tuple-element.265, f32[592,1024]{1,0:T(8,128)S(1)} %copy-done.8, f32[1024]{0:T(1024)S(1)} %add.334, f32[1024]{0:T(1024)S(1)} %mul.440, f32[592]{0:T(1024)S(1)} %add_rsqrt_fusion, f32[592]{0:T(1024)S(1)} %broadcast_multiply_fusion.4), kind=kOutput, calls=%fused_computation.13 | convolution fusion | flops 4973281280 | bytes 15676032 | tf_op jit(solution)/shard_map/icd,icf->df/dot_general | solution.py:322
  325.0 14.5 %reshape.707 = bf16[16,64,2,4,512]{4,3,2,1,0:T(4,128)(2,1)} reshape(bf16[1024,4096]{1,0:T(8,128)(2,1)} %convolution_convert_fusion) | data formatting | bytes 16777216 | tf_op jit(solution)/shard_map/reshape | solution.py:374
  339.5 13.0 %copy.240 = bf16[16,64,2,4,512]{4,2,1,3,0:T(2,128)(2,1)} copy(bf16[16,64,2,4,512]{4,3,2,1,0:T(4,128)(2,1)} %reshape.707) | data formatting | bytes 16777216 | tf_op jit(solution)/shard_map/reshape | solution.py:374
  352.6 14.3 %reshape.708 = bf16[16,256,1024]{2,1,0:T(8,128)(2,1)} reshape(bf16[16,4,64,2,512]{4,3,2,1,0:T(2,128)(2,1)} %bitcast.92) | data formatting | bytes 16777216 | tf_op jit(solution)/shard_map/reshape | solution.py:376
  366.8 9.1 %convolution_convert_fusion.1 = bf16[4096,1024]{1,0:T(8,128)(2,1)S(1)} fusion(bf16[592,4096]{1,0:T(8,128)(2,1)} %get-tuple-element.260, f32[592]{0:T(1024)S(1)} %fusion.52, bf16[296,1024]{1,0:T(8,128)(2,1)} %bitcast.19, bf16[296,1024]{1,0:T(8,128)(2,1)S(1)} %bitcast.117), kind=kOutput, calls=%fused_computation.14 | convolution fusion | flops 4973887488 | bytes 14453056 | tf_op jit(solution)/shard_map/icf,icd->fd/dot_general | solution.py:317
  375.9 2.3 fusion.68
  378.2 1.9 convolution_convert_fusion.3
  380.1 1.2 slice-done.1
  381.3 16.6 %pad_maximum_fusion = bf16[16,576,1024]{2,1,0:T(8,128)(2,1)} fusion(bf16[16,256,1024]{2,1,0:T(8,128)(2,1)S(1)} %bitcast.108, bf16[16,256,1024]{2,1,0:T(8,128)(2,1)S(1)} %bitcast.94, bf16[16,64,1024]{2,1,0:T(8,128)(2,1)S(1)} %bitcast.119), kind=kLoop, calls=%fused_computation | loop fusion | flops 56623104 | bytes 37748736 | tf_op jit(solution)/shard_map/concatenate | solution.py:370
  399.5 1.6 multiply_reduce_fusion
  401.1 4.5 fusion.30.g_ref
  405.6 33.4 %shard_map.396 = (f32[1,592,1024]{2,1,0:T(8,128)}, f32[1,592,1024]{2,1,0:T(8,128)}, f32[1,592,1024]{2,1,0:T(8,128)}) custom-call(bf16[1,592,1024]{2,1,0:T(8,128)(2,1)} %copy-done.2, bf16[1,592,1024]{2,1,0:T(8,128)(2,1)} %copy-done, bf16[1,592,1024]{2,1,0:T(8,128)(2,1)} %copy-done.1, bf16[1,592,1024]{2,1,0:T(8,128)(2,1)} %fusion.30.g_ref, ...), custom_call_target="tpu_custom_call" | custom-call | flops 7177502720 | bytes 12124160 | tf_op jit(solution)/shard_map/pallas_call | solution.py:135
  439.0 4.6 fusion.69
  443.7 2.8 convert_bitcast_fusion.1
  446.6 5.7 fusion.20
  452.8 7.6 %convolution_convert_fusion.2 = bf16[1024,3072]{1,0:T(8,128)(2,1)S(1)} fusion(bf16[592,1024]{1,0:T(8,128)(2,1)} %copy-done.27, bf16[592,1024]{1,0:T(8,128)(2,1)} %copy-done.29, bf16[592,1024]{1,0:T(8,128)(2,1)} %copy-done.28, f32[1024]{0:T(1024)S(1)} %copy-done.58, f32[1024]{0:T(1024)S(1)} %copy-done.54, f32[592]{0:T(1024)S(1)} %copy-done.56, ...), kind=kOutput, calls=%fused_computation.17 | convolution fusion | flops 3744055296 | bytes 11154048 | tf_op jit(solution)/shard_map/icd,ice->de/dot_general | solution.py:344
  460.3 3.1 fusion.6
  463.4 126.9 %reduce-scatter.5.cloned.1.call-done = bf16[576,1024]{1,0:T(8,128)(2,1)} async-done(((bf16[9216,1024]{1,0:T(8,128)(2,1)}), bf16[576,1024]{1,0:T(8,128)(2,1)}) %reduce-scatter.5.cloned.1.call-update) | async-done | bytes 1179664 | tf_op jit(solution)/shard_map/reduce_scatter | solution.py:381
  590.5 10.8 %fusion.31 = bf16[1,592,1024]{2,1,0:T(8,128)(2,1)S(1)} fusion(f32[592,1024]{1,0:T(8,128)} %copy-done.7, bf16[592,4096]{1,0:T(8,128)(2,1)} %get-tuple-element.260, bf16[4096,1024]{0,1:T(8,128)(2,1)} %bitcast.104, f32[1024]{0:T(1024)S(1)} %add.342), kind=kOutput, calls=%fused_computation.68 | convolution fusion | flops 4967874560 | bytes 16879616 | tf_op jit(solution)/shard_map/icf,fd->icd/dot_general | solution.py:312
  602.4 1.5 collective-permute-start.1
  604.0 1.4 fusion.35
  607.6 1.5 collective-permute-start.3
  611.1 1.3 copy.215
  612.5 6.8 collective-permute-done.1
  619.2 1.9 constant_dynamic-update-slice_fusion.1
  621.2 11.0 %collective-permute-done.3 = bf16[1,296,1024]{2,1,0:T(8,128)(2,1)S(1)} collective-permute-done((bf16[1,296,1024]{2,1,0:T(8,128)(2,1)}, bf16[1,296,1024]{2,1,0:T(8,128)(2,1)S(1)}, u32[]{:S(2)}, u32[]{:S(2)}) %collective-permute-start.3) | collective-permute-done | bytes 606240 | tf_op jit(solution)/shard_map/ppermute | solution.py:177
  633.0 10.6 %collective-permute-done.5 = bf16[576,512]{1,0:T(8,128)(2,1)} collective-permute-done((bf16[576,512]{1,0:T(8,128)(2,1)}, bf16[576,512]{1,0:T(8,128)(2,1)}, u32[]{:S(2)}, u32[]{:S(2)}) %collective-permute-start.5) | collective-permute-done | bytes 589856 | tf_op jit(solution)/shard_map/ppermute | solution.py:191
  643.6 1.3 convert_add_fusion.1
  645.0 1.5 multiply_subtract_fusion.1
  647.5 1.4 multiply_subtract_fusion.2
  648.9 31.1 %reduce-scatter.7.cloned.1.call-done = bf16[64,3200]{1,0:T(8,128)(2,1)} async-done(((bf16[1024,3200]{1,0:T(8,128)(2,1)}), bf16[64,3200]{1,0:T(8,128)(2,1)}) %reduce-scatter.7.cloned.1.call-update) | async-done | bytes 409616
  681.5 1.5 collective-permute-start.6
  683.0 1.0 slice.167
  686.5 1.3 multiply_subtract_fusion.4
  687.8 1.3 multiply_subtract_fusion.5
  689.1 5.1 collective-permute-done.4
  694.2 2.6 multiply_subtract_fusion
  696.8 2.2 copy.218
  699.0 2.1 copy.219
  (214 shorter events, 26.7 us)
Async XLA Ops:
  7.2 5.6 copy-start.40
  7.2 77.9 %all-gather.3.cloned.1.call-start = ((), (), s32[]{:S(2)}) async-start(), calls=%async_computation.2 | async-start | bytes 7028736 | tf_op jit(solution)/shard_map/all_gather | solution.py:234
  9.8 75.4 %copy-start.30 = (bf16[2,296,1024]{2,1,0:T(8,128)(2,1)S(1)}, bf16[2,296,1024]{2,1,0:T(8,128)(2,1)}, u32[]{:S(2)}) copy-start(bf16[2,296,1024]{2,1,0:T(8,128)(2,1)} %param.20) | copy-start | bytes 3637252
  10.5 203.1 %all-gather.5.cloned.1.call-start = ((), (), s32[]{:S(2)}) async-start(), calls=%async_computation.3 | async-start | bytes 19464192 | tf_op jit(solution)/shard_map/all_gather | solution.py:247
  12.8 74.9 %copy-start.31 = (bf16[2,296,1024]{2,1,0:T(8,128)(2,1)S(1)}, bf16[2,296,1024]{2,1,0:T(8,128)(2,1)}, u32[]{:S(2)}) copy-start(bf16[2,296,1024]{2,1,0:T(8,128)(2,1)} %param.21) | copy-start | bytes 3637252
  85.2 505.2 %reduce-scatter.5.cloned.1.call-start = ((), (), s32[]{:S(2)}) async-start(), calls=%async_computation.4 | async-start | bytes 20054016 | tf_op jit(solution)/shard_map/reduce_scatter | solution.py:381
  86.2 21.0 %collective-permute-start = (bf16[1,296,1024]{2,1,0:T(8,128)(2,1)}, bf16[1,296,1024]{2,1,0:T(8,128)(2,1)S(1)}, u32[]{:S(2)}, u32[]{:S(2)}) collective-permute-start(bf16[1,296,1024]{2,1,0:T(8,128)(2,1)} %get-tuple-element.243), channel_id=1, source_target_pairs={{0,1},{1,0},{2,3},{3,2},{4,5},{5,4},{6,7},{7,6},{8,9},{9,8},{10,11... | collective-permute-start | bytes 1818632 | tf_op jit(solution)/shard_map/ppermute | solution.py:164
  88.8 204.6 %collective-permute-start.2 = (bf16[1,296,1024]{2,1,0:T(8,128)(2,1)}, bf16[1,296,1024]{2,1,0:T(8,128)(2,1)}, u32[]{:S(2)}, u32[]{:S(2)}) collective-permute-start(bf16[1,296,1024]{2,1,0:T(8,128)(2,1)} %get-tuple-element.239), channel_id=1, source_target_pairs={{0,1},{1,0},{2,3},{3,2},{4,5},{5,4},{6,7},{7,6},{8,9},{9,8},{10,11... | collective-permute-start | bytes 1818632 | tf_op jit(solution)/shard_map/ppermute | solution.py:164
  89.3 18.5 %copy-start.48 = (s32[296]{0:T(512)}, s32[296]{0:T(512)S(1)}, u32[]{:S(2)}) copy-start(s32[296]{0:T(512)S(1)} %iota_add_fusion) | copy-start | bytes 3556
  89.3 18.5 %copy-start.50 = (s32[296]{0:T(512)}, s32[296]{0:T(512)S(1)}, u32[]{:S(2)}) copy-start(s32[296]{0:T(512)S(1)} %iota_add_fusion.1) | copy-start | bytes 3556
  107.1 6.5 copy-start.10
  107.4 6.2 copy-start.46
  107.9 5.7 copy-start.55
  110.0 3.6 copy-start.57
  110.1 3.5 copy-start.53
  113.6 4.2 copy-start.17
  113.6 4.2 copy-start.19
  117.8 3.0 copy-start.15
  120.9 3.5 copy-start
  124.5 17.3 %copy-start.1 = (bf16[1,592,1024]{2,1,0:T(8,128)(2,1)}, bf16[1,592,1024]{2,1,0:T(8,128)(2,1)S(1)}, u32[]{:S(2)}) copy-start(bf16[1,592,1024]{2,1,0:T(8,128)(2,1)S(1)} %get-tuple-element.228.v_ref) | copy-start | bytes 3637252
  236.4 14.5 %copy-start.4 = (bf16[1,592,1024]{2,1,0:T(8,128)(2,1)S(1)}, bf16[1,592,1024]{2,1,0:T(8,128)(2,1)}, u32[]{:S(2)}) copy-start(bf16[1,592,1024]{2,1,0:T(8,128)(2,1)} %copy-done.3) | copy-start | bytes 3637252
  236.4 14.5 %copy-start.11 = (bf16[1,296,1024]{2,1,0:T(8,128)(2,1)S(1)}, bf16[1,296,1024]{2,1,0:T(8,128)(2,1)}, u32[]{:S(2)}) copy-start(bf16[1,296,1024]{2,1,0:T(8,128)(2,1)} %copy-done.10) | copy-start | bytes 1818628
  250.9 3.7 slice-start.2
  250.9 4.1 slice-start.3
  254.2 11.8 %copy-start.7 = (f32[592,1024]{1,0:T(8,128)}, f32[592,1024]{1,0:T(8,128)S(1)}, u32[]{:S(2)}) copy-start(f32[592,1024]{1,0:T(8,128)S(1)} %get-tuple-element.259) | copy-start | bytes 7274500
  281.0 12.4 %copy-start.14 = (bf16[1,296,1024]{2,1,0:T(8,128)(2,1)S(1)}, bf16[1,296,1024]{2,1,0:T(8,128)(2,1)}, u32[]{:S(2)}) copy-start(bf16[1,296,1024]{2,1,0:T(8,128)(2,1)} %get-tuple-element.238) | copy-start | bytes 1818628
  293.4 12.3 %copy-start.8 = (f32[592,1024]{1,0:T(8,128)S(1)}, f32[592,1024]{1,0:T(8,128)}, u32[]{:S(2)}) copy-start(f32[592,1024]{1,0:T(8,128)} %copy-done.7) | copy-start | bytes 7274500
  366.8 9.1 %copy-start.9 = (f32[592,1024]{1,0:T(8,128)S(1)}, f32[592,1024]{1,0:T(8,128)}, u32[]{:S(2)}) copy-start(f32[592,1024]{1,0:T(8,128)} %copy-done.7) | copy-start | bytes 7274500
  366.8 9.1 %copy-start.22 = (f32[592,1024]{1,0:T(8,128)S(1)}, f32[592,1024]{1,0:T(8,128)}, u32[]{:S(2)}) copy-start(f32[592,1024]{1,0:T(8,128)} %get-tuple-element.262) | copy-start | bytes 7274500
  375.9 4.2 slice-start
  378.2 1.9 copy-start.5
  378.2 3.1 slice-start.1
  397.9 3.2 copy-start.6
  397.9 282.1 %reduce-scatter.7.cloned.1.call-start = ((), (), s32[]{:S(2)}) async-start(), calls=%async_computation.5 | async-start | bytes 6963200
  439.0 7.6 %copy-start.18 = (bf16[1024,1536]{1,0:T(8,128)(2,1)S(1)}, bf16[1024,1536]{1,0:T(8,128)(2,1)}, u32[]{:S(2)}) copy-start(bf16[1024,1536]{1,0:T(8,128)(2,1)} %copy-done.17) | copy-start | bytes 9437188
  439.0 7.6 %copy-start.20 = (bf16[1024,1536]{1,0:T(8,128)(2,1)S(1)}, bf16[1024,1536]{1,0:T(8,128)(2,1)}, u32[]{:S(2)}) copy-start(bf16[1024,1536]{1,0:T(8,128)(2,1)} %copy-done.19) | copy-start | bytes 9437188
  443.7 8.7 %copy-start.27 = (bf16[592,1024]{1,0:T(8,128)(2,1)}, bf16[592,1024]{1,0:T(8,128)(2,1)S(1)}, u32[]{:S(2)}) copy-start(bf16[592,1024]{1,0:T(8,128)(2,1)S(1)} %get-tuple-element.233) | copy-start | bytes 3637252
  443.7 8.7 %copy-start.28 = (bf16[592,1024]{1,0:T(8,128)(2,1)}, bf16[592,1024]{1,0:T(8,128)(2,1)S(1)}, u32[]{:S(2)}) copy-start(bf16[592,1024]{1,0:T(8,128)(2,1)S(1)} %get-tuple-element.266) | copy-start | bytes 3637252
  443.7 2.9 copy-start.12
  443.7 2.9 copy-start.47
  443.7 2.9 copy-start.54
  443.7 2.9 copy-start.56
  446.6 5.8 copy-start.29
  446.6 6.1 copy-start.58
  463.4 127.0 %copy-start.45 = (f32[1,16,2,32]{3,2,1,0:T(2,128)S(1)}, f32[1,16,2,32]{3,2,1,0:T(2,128)}, u32[]{:S(2)}) copy-start(f32[1,16,2,32]{3,2,1,0:T(2,128)} %get-tuple-element.248) | copy-start | bytes 12292
  601.3 2.6 copy-start.13
  601.3 2.7 copy-start.21
  602.4 16.9 %collective-permute-start.1 = (bf16[1,296,1024]{2,1,0:T(8,128)(2,1)}, bf16[1,296,1024]{2,1,0:T(8,128)(2,1)}, u32[]{:S(2)}, u32[]{:S(2)}) collective-permute-start(bf16[1,296,1024]{2,1,0:T(8,128)(2,1)} %get-tuple-element.240), channel_id=1, source_target_pairs={{0,1},{1,0},{2,3},{3,2},{4,5},{5,4},{6,7},{7,6},{8,9},{9,8},{10,11... | collective-permute-start | bytes 1818632 | tf_op jit(solution)/shard_map/ppermute | solution.py:177
  605.4 3.6 copy-start.34
  605.4 5.1 copy-start.26
  605.6 5.2 copy-start.42
  607.6 24.6 %collective-permute-start.3 = (bf16[1,296,1024]{2,1,0:T(8,128)(2,1)}, bf16[1,296,1024]{2,1,0:T(8,128)(2,1)S(1)}, u32[]{:S(2)}, u32[]{:S(2)}) collective-permute-start(bf16[1,296,1024]{2,1,0:T(8,128)(2,1)} %get-tuple-element.236), channel_id=1, source_target_pairs={{0,1},{1,0},{2,3},{3,2},{4,5},{5,4},{6,7},{7,6},{8,9},{9,8},{10,11... | collective-permute-start | bytes 1818632 | tf_op jit(solution)/shard_map/ppermute | solution.py:177
  610.0 33.6 %collective-permute-start.5 = (bf16[576,512]{1,0:T(8,128)(2,1)}, bf16[576,512]{1,0:T(8,128)(2,1)}, u32[]{:S(2)}, u32[]{:S(2)}) collective-permute-start(bf16[576,512]{1,0:T(8,128)(2,1)} %constant_dynamic-slice_fusion.2), channel_id=1, source_target_pairs={{0,1},{1,0},{2,3},{3,2},{4,5},{5,4},{6,7},{7,6},{8,9},{9,8},{10,11... | collective-permute-start | bytes 1769480 | tf_op jit(solution)/shard_map/ppermute | solution.py:191
  612.4 32.5 %copy-start.23 = (f32[256,512]{1,0:T(8,128)S(1)}, f32[256,512]{1,0:T(8,128)}, u32[]{:S(2)}) copy-start(f32[256,512]{1,0:T(8,128)} %param.25) | copy-start | bytes 1572868
  612.4 31.2 %copy-start.35 = (bf16[576,1024]{1,0:T(8,128)(2,1)S(1)}, bf16[576,1024]{1,0:T(8,128)(2,1)}, u32[]{:S(2)}) copy-start(bf16[576,1024]{1,0:T(8,128)(2,1)} %reduce-scatter.5.cloned.1.call-done) | copy-start | bytes 3538948
  612.4 32.4 %copy-start.36 = (f32[256,512]{1,0:T(8,128)S(1)}, f32[256,512]{1,0:T(8,128)}, u32[]{:S(2)}) copy-start(f32[256,512]{1,0:T(8,128)} %param.31) | copy-start | bytes 1572868
  612.5 32.4 %copy-start.37 = (f32[256,512]{1,0:T(8,128)S(1)}, f32[256,512]{1,0:T(8,128)}, u32[]{:S(2)}) copy-start(f32[256,512]{1,0:T(8,128)} %param.37) | copy-start | bytes 1572868
  644.9 2.6 copy-start.24
  645.0 2.5 copy-start.38
  645.0 2.5 copy-start.39
  647.5 39.0 %copy-start.52 = (f32[10,32]{1,0:T(8,128)S(1)}, f32[10,32]{1,0:T(8,128)}, u32[]{:S(2)}) copy-start(f32[10,32]{1,0:T(8,128)} %param.27) | copy-start | bytes 3844
  681.5 4.2 collective-permute-start.6
  684.3 9.9 %collective-permute-start.4 = (bf16[64,1536]{0,1:T(8,128)(2,1)S(1)}, bf16[64,1536]{0,1:T(8,128)(2,1)}, u32[]{:S(2)}, u32[]{:S(2)}) collective-permute-start(bf16[64,1536]{0,1:T(8,128)(2,1)S(1)} %copy.227), channel_id=1, source_target_pairs={{0,1},{1,0},{2,3},{3,2},{4,5},{5,4},{6,7},{7,6},{8,9},{9,8},{10,11... | collective-permute-start | bytes 589832 | tf_op jit(solution)/shard_map/ppermute | solution.py:191
  696.8 4.3 copy-start.16
  (10 other events, 11.7 us)
Sparse Core Ops, SparseCore 0:
  11.5 73.6 all-gather.2
  88.0 125.5 all-gather.4
  398.0 192.2 reduce-scatter.4
  594.1 85.8 reduce-scatter.6
where the time goes:
time: 717 us; the launch traced here: 710 us
  waiting for transfers between devices  351 us (49%)
  local copies, waits for them, and re-layouts  141 us (20%)
  matrix products  89.5 us (12%)
  other arithmetic  55.1 us (8%)
  Pallas kernels  50.7 us (7%)
  between operations  15.1 us (2%)
  starting transfers between devices  7.78 us (1%)
    reduce_scatter x1, waiting for transfers between devices, body(): part = lax.psum_scatter(send_a, 'dp', scatter_dimension=0, tiled=True)  127 us
    all_gather x1, waiting for transfers between devices, body(): wide_a = lax.all_gather(part_a, ('seq', 'dp'), axis=0, tiled=True)  71.5 us
    all_gather x1, waiting for transfers between devices, body(): wide_b = lax.all_gather(part_b, ('seq', 'dp'), axis=0, tiled=True)  69.8 us
    reshape x3, local copies, waits for them, and re-layouts, body(): send_a = jnp.concatenate([g_outw.astype(jnp.bfloat16).reshape(blocks, row...  41.8 us
    pallas_call x1, Pallas kernels, attend_back(): pl.pallas_call(attend_back_kernel, grid=(count, width // LANES), in_specs...  33.4 us
    unnamed x141, local copies, waits for them, and re-layouts  32.9 us
    unnamed x5, waiting for transfers between devices  31.2 us
    transpose x2, local copies, waits for them, and re-layouts, body(): wide_b[:, :, (1 + fold) * rows_dp:].transpose(1, 2, 0, 3)  24.3 us
  transfers between devices with their start and end apart: 11, of which 10 were waited for; matrix products, arithmetic and copies ran while one was open for 23% of the time, Pallas kernels for 7%

commit v1 on v0

--- a/solution.py
+++ b/solution.py
@@ -1,3 +1,5 @@
+import functools
+
 import jax
 import jax.numpy as jnp
 from jax import lax
@@ -192,7 +194,318 @@
     return total
 
 
-def body(
+MESH = pl.DeviceIdType.MESH
+
+
+def place():
+    d = lax.axis_index("dp")
+    return lax.rem(d, 2), lax.rem(d // 2, 2), d // 4, lax.axis_index("seq")
+
+
+def greet(core, x, z, y, depth):
+    barrier = pltpu.get_barrier_semaphore()
+    others = [site(core, x, lax.rem(z + k, depth), y) for k in range(1, depth)]
+    others += [site(core, 1 - x, z, y), site(core, x, z, 1 - y), site(1 - core, x, z, y)]
+    for other in others:
+        pl.semaphore_signal(barrier, inc=1, device_id=other, device_id_type=MESH)
+    pl.semaphore_wait(barrier, len(others))
+
+
+def site(core, x, z, y):
+    return {"dp": (z * 2 + x) * 2 + core, "seq": y}
+
+
+def columns(index, size):
+    return pl.ds(pl.multiple_of(index * size, LANES), size)
+
+
+def gather_kernel(parts, depth, count, *refs):
+    shards, outs = refs[:count], refs[count : 2 * count]
+    own_sem, send, recv = refs[2 * count :]
+    core, x, z, y = place()
+    greet(core, x, z, y, depth)
+    pending = []
+
+    def push(src, dst, p, lane, target):
+        copy = pltpu.make_async_remote_copy(
+            src_ref=src,
+            dst_ref=dst,
+            send_sem=send.at[p, lane],
+            recv_sem=recv.at[p, lane],
+            device_id=target,
+            device_id_type=MESH,
+        )
+        copy.start()
+        pending.append(copy)
+        return copy
+
+    def view(p):
+        w, start, size, kind = parts[p]
+        return shards[w].at[start : start + size], outs[w], pl.ds(start, size), shards[w].shape[1], kind
+
+    state = {}
+
+    def stage0(p):
+        src, out, rows, width, kind = view(p)
+        mine = out.at[z, x, core, rows, columns(y, width)]
+        local = pltpu.make_async_copy(src, mine, own_sem.at[p])
+        local.start()
+        state[p] = [local] + [
+            push(src, mine, p, k - 1, site(core, x, lax.rem(z + k, depth), y))
+            for k in range(1, depth)
+        ]
+
+    def stage1(p):
+        src, out, rows, width, kind = view(p)
+        state[p][0].wait()
+        for copy in state[p][1:]:
+            copy.wait_recv()
+        block = out.at[:, x, core, rows, columns(y, width)]
+        target = site(core, 1 - x, z, y) if kind == 0 else site(core, x, z, 1 - y)
+        state[p] = push(block, block, p, depth - 1, target)
+
+    def stage2(p):
+        src, out, rows, width, kind = view(p)
+        state[p].wait_recv()
+        if kind == 0:
+            block = out.at[:, :, core, rows, columns(y, width)]
+            state[p] = push(block, block, p, depth, site(core, x, z, 1 - y))
+        else:
+            block = out.at[:, x, core, rows, :]
+            state[p] = push(block, block, p, depth, site(core, 1 - x, z, y))
+
+    def stage3(p):
+        src, out, rows, width, kind = view(p)
+        state[p].wait_recv()
+        block = out.at[:, :, core, rows, :]
+        state[p] = push(block, block, p, depth + 1, site(1 - core, x, z, y))
+
+    def stage4(p):
+        state[p].wait_recv()
+
+    total = len(parts)
+    for p in range(total):
+        stage0(p)
+    for step in range(total // 2 + 3):
+        for lag, stage in enumerate((stage1, stage2, stage3, stage4)):
+            for p in (2 * (step - lag), 2 * (step - lag) + 1):
+                if 0 <= p < total:
+                    stage(p)
+    for copy in pending:
+        copy.wait_send()
+
+
+def split_rows(shapes, pieces):
+    parts = []
+    for w, (shape, n) in enumerate(zip(shapes, pieces)):
+        size = shape[0] // n
+        parts += [(w, i * size, size, i % 2) for i in range(n)]
+    return parts
+
+
+def gather(shards, pieces, cid, depth):
+    parts = split_rows([s.shape for s in shards], pieces)
+    total = len(parts)
+    outs = pl.pallas_call(
+        functools.partial(gather_kernel, parts, depth, len(shards)),
+        in_specs=[pl.BlockSpec(memory_space=pltpu.VMEM)] * len(shards),
+        out_specs=[pl.BlockSpec(memory_space=pl.ANY)] * len(shards),
+        out_shape=[
+            jax.ShapeDtypeStruct((depth, 2, 2, s.shape[0], 2 * s.shape[1]), s.dtype) for s in shards
+        ],
+        scratch_shapes=[
+            pltpu.SemaphoreType.DMA((total,)),
+            pltpu.SemaphoreType.DMA((total, depth + 2)),
+            pltpu.SemaphoreType.DMA((total, depth + 2)),
+        ],
+        compiler_params=pltpu.CompilerParams(collective_id=cid, has_side_effects=True),
+    )(*shards)
+    return [o.reshape(-1, o.shape[-1]) for o in outs]
+
+
+def reduce_kernel(parts, depth, count, shapes, *refs):
+    grads, outs = refs[:count], refs[count : 2 * count]
+    own, near = refs[2 * count : 3 * count], refs[3 * count : 4 * count]
+    mid, side, far, last = (refs[i * count : (i + 1) * count] for i in (4, 5, 6, 7))
+    own_sem, send, recv = refs[8 * count :]
+    core, x, z, y = place()
+    greet(core, x, z, y, depth)
+    pending = []
+
+    def push(src, dst, p, lane, target):
+        copy = pltpu.make_async_remote_copy(
+            src_ref=src,
+            dst_ref=dst,
+            send_sem=send.at[p, lane],
+            recv_sem=recv.at[p, lane],
+            device_id=target,
+            device_id_type=MESH,
+        )
+        copy.start()
+        pending.append(copy)
+        return copy
+
+    def view(p):
+        w, start, size, kind = parts[p]
+        return w, pl.ds(start, size), shapes[w][1], kind
+
+    state = {}
+
+    def add(left, right):
+        return left[...].astype(jnp.float32) + right[...].astype(jnp.float32)
+
+    def stage0(p):
+        w, rows, width, kind = view(p)
+        local = pltpu.make_async_copy(
+            grads[w].at[:, :, core, rows], own[w].at[:, :, rows], own_sem.at[p]
+        )
+        local.start()
+        copy = push(
+            grads[w].at[:, :, 1 - core, rows],
+            near[w].at[:, :, rows],
+            p,
+            depth - 1,
+            site(1 - core, x, z, y),
+        )
+        state[p] = (local, copy)
+
+    def stage1(p):
+        w, rows, width, kind = view(p)
+        local, copy = state[p]
+        local.wait()
+        copy.wait_recv()
+
+        def body(i, carry):
+            mine = own[w].at[i // 2, lax.rem(i, 2), rows]
+            mine[...] = add(mine, near[w].at[i // 2, lax.rem(i, 2), rows]).astype(jnp.bfloat16)
+            return carry
+
+        lax.fori_loop(0, 2 * depth, body, 0)
+        if kind == 0:
+            state[p] = push(
+                own[w].at[:, :, rows, columns(1 - y, width)],
+                mid[w].at[:, :, rows],
+                p,
+                depth,
+                site(core, x, z, 1 - y),
+            )
+        else:
+            state[p] = push(
+                own[w].at[:, 1 - x, rows],
+                side[w].at[:, rows],
+                p,
+                depth,
+                site(core, 1 - x, z, y),
+            )
+
+    def stage2(p):
+        w, rows, width, kind = view(p)
+        state[p].wait_recv()
+        if kind == 0:
+
+            def body(i, carry):
+                mine = own[w].at[i // 2, lax.rem(i, 2), rows, columns(y, width)]
+                mine[...] = add(mine, mid[w].at[i // 2, lax.rem(i, 2), rows]).astype(jnp.bfloat16)
+                return carry
+
+            lax.fori_loop(0, 2 * depth, body, 0)
+            state[p] = push(
+                own[w].at[:, 1 - x, rows, columns(y, width)],
+                far[w].at[:, rows],
+                p,
+                depth + 1,
+                site(core, 1 - x, z, y),
+            )
+        else:
+
+            def body(i, carry):
+                mine = own[w].at[i, x, rows]
+                mine[...] = add(mine, side[w].at[i, rows]).astype(jnp.bfloat16)
+                return carry
+
+            lax.fori_loop(0, depth, body, 0)
+            state[p] = push(
+                own[w].at[:, x, rows, columns(1 - y, width)],
+                far[w].at[:, rows],
+                p,
+                depth + 1,
+                site(core, x, z, 1 - y),
+            )
+
+    def stage3(p):
+        w, rows, width, kind = view(p)
+        state[p].wait_recv()
+
+        def body(i, carry):
+            mine = own[w].at[i, x, rows, columns(y, width)]
+            mine[...] = add(mine, far[w].at[i, rows]).astype(jnp.bfloat16)
+            return carry
+
+        lax.fori_loop(0, depth, body, 0)
+        state[p] = [
+            push(
+                own[w].at[lax.rem(z + k, depth), x, rows, columns(y, width)],
+                last[w].at[k - 1, rows],
+                p,
+                k - 1,
+                site(core, x, lax.rem(z + k, depth), y),
+            )
+            for k in range(1, depth)
+        ]
+
+    def stage4(p):
+        w, rows, width, kind = view(p)
+        for copy in state[p]:
+            copy.wait_recv()
+        total = own[w][z, x, rows, columns(y, width)].astype(jnp.float32)
+        for k in range(depth - 1):
+            total = total + last[w][k, rows].astype(jnp.float32)
+        outs[w][rows] = total
+
+    total = len(parts)
+    for p in range(total):
+        stage0(p)
+    for step in range(total // 2 + 4):
+        for lag, stage in enumerate((stage1, stage2, stage3, stage4)):
+            for p in (2 * (step - lag), 2 * (step - lag) + 1):
+                if 0 <= p < total:
+                    stage(p)
+    for copy in pending:
+        copy.wait_send()
+
+
+def reduce_sum(grads, pieces, cid, depth):
+    count = len(grads)
+    shapes = [(g.shape[0] // (4 * depth), g.shape[1] // 2) for g in grads]
+    parts = split_rows(shapes, pieces)
+    total = len(parts)
+
+    def each(form):
+        return [pltpu.VMEM(form(r, c), jnp.bfloat16) for r, c in shapes]
+
+    return pl.pallas_call(
+        functools.partial(reduce_kernel, parts, depth, count, shapes),
+        in_specs=[pl.BlockSpec(memory_space=pl.ANY)] * count,
+        out_specs=[pl.BlockSpec(memory_space=pltpu.VMEM)] * count,
+        out_shape=[jax.ShapeDtypeStruct(s, jnp.float32) for s in shapes],
+        scratch_shapes=each(lambda r, c: (depth, 2, r, 2 * c))
+        + each(lambda r, c: (depth, 2, r, 2 * c))
+        + each(lambda r, c: (depth, 2, r, c))
+        + each(lambda r, c: (depth, r, 2 * c))
+        + each(lambda r, c: (depth, r, c))
+        + each(lambda r, c: (depth - 1, r, c))
+        + [
+            pltpu.SemaphoreType.DMA((total,)),
+            pltpu.SemaphoreType.DMA((total, depth + 2)),
+            pltpu.SemaphoreType.DMA((total, depth + 2)),
+        ],
+        compiler_params=pltpu.CompilerParams(
+            collective_id=cid, has_side_effects=True, vmem_limit_bytes=56 * 1024 * 1024
+        ),
+    )(*[g.reshape(depth, 2, 2, r, 2 * c) for g, (r, c) in zip(grads, shapes)])
+
+
+def general_body(
     images,
     cotangent,
     w_qkv,
@@ -435,7 +748,193 @@
     )
 
 
+def is_paired(mesh):
+    return mesh.shape["seq"] == 2 and mesh.shape["dp"] % 4 == 0
+
+
+def attend_mixed_kernel(q_ref, k_ref, v_ref, live_ref, ctx_ref):
+    attend_kernel(q_ref, k_ref, v_ref, live_ref, ctx_ref)
+
+
+def attend_mixed(mixed, live):
+    count, rows, triple = mixed.shape
+    width = triple // 3
+    heads = width // LANES
+    specs = [
+        pl.BlockSpec((1, rows, LANES), lambda i, h, k=k: (i, 0, h + k * heads)) for k in range(3)
+    ]
+    pairs = count * rows * rows * width
+    return pl.pallas_call(
+        attend_mixed_kernel,
+        grid=(count, heads),
+        in_specs=specs + [pl.BlockSpec((1, rows), lambda i, h: (0, 0))],
+        out_specs=specs[0],
+        out_shape=jax.ShapeDtypeStruct((count, rows, width), jnp.bfloat16),
+        cost_estimate=pl.CostEstimate(
+            flops=8 * pairs, bytes_accessed=2 * mixed.size, transcendentals=pairs // HEAD_DIM
+        ),
+        compiler_params=pltpu.CompilerParams(vmem_limit_bytes=48 * 1024 * 1024),
+    )(mixed, mixed, mixed, live.reshape(1, rows))
+
+
+def attend_back_mixed_kernel(q_ref, k_ref, v_ref, g_ref, live_ref, dm_ref, sum_ref, dq, dk, dv):
+    attend_back_kernel(q_ref, k_ref, v_ref, g_ref, live_ref, dq, dk, dv)
+    image, head = pl.program_id(0), pl.program_id(1)
+    width = dm_ref.shape[2] // 3
+
+    @pl.when(jnp.logical_and(image == 0, head == 0))
+    def _():
+        sum_ref[...] = jnp.zeros_like(sum_ref)
+
+    for k, part in enumerate((dq, dk, dv)):
+        where = pl.ds(pl.multiple_of(k * width + head * LANES, LANES), LANES)
+        dm_ref[0, :, where] = part[0].astype(jnp.bfloat16)
+        sum_ref[:, where] += jnp.sum(part[0], axis=0, keepdims=True)
+
+
+def attend_back_mixed(mixed, grad_ctx, live):
+    count, rows, triple = mixed.shape
+    width = triple // 3
+    heads = width // LANES
+    specs = [
+        pl.BlockSpec((1, rows, LANES), lambda i, h, k=k: (i, 0, h + k * heads)) for k in range(3)
+    ]
+    pairs = count * rows * rows * width
+    return pl.pallas_call(
+        attend_back_mixed_kernel,
+        grid=(count, heads),
+        in_specs=specs + [specs[0], pl.BlockSpec((rows, 1), lambda i, h: (0, 0))],
+        out_specs=[
+            pl.BlockSpec((1, rows, triple), lambda i, h: (i, 0, 0)),
+            pl.BlockSpec((1, triple), lambda i, h: (0, 0)),
+        ],
+        out_shape=[
+            jax.ShapeDtypeStruct(mixed.shape, jnp.bfloat16),
+            jax.ShapeDtypeStruct((1, triple), jnp.float32),
+        ],
+        scratch_shapes=[pltpu.VMEM((1, rows, LANES), jnp.float32)] * 3,
+        cost_estimate=pl.CostEstimate(
+            flops=20 * pairs, bytes_accessed=4 * mixed.size, transcendentals=pairs // HEAD_DIM
+        ),
+        compiler_params=pltpu.CompilerParams(vmem_limit_bytes=56 * 1024 * 1024),
+    )(mixed, mixed, mixed, grad_ctx, live.reshape(rows, 1))
+
+
+def product(a, b, dims=NN):
+    return lax.dot_general(a, b, dims, preferred_element_type=jnp.float32)
+
+
+def fast_body(images, cotangent, *rest):
+    params, firsts, seconds = rest[:6], rest[6:12], rest[12:]
+    w_qkv, w_out, w_up, w_down, gains, biases = params
+    count, group, width = images.shape
+    ways = lax.axis_size("seq")
+    blocks = lax.axis_size("dp")
+    depth = blocks // 4
+    me = lax.axis_index("seq")
+    narrow = jnp.bfloat16
+    vectors = gains.shape[0] + biases.shape[0]
+    own = gains.shape[1]
+    lanes = -(-own // LANES) * LANES
+    tall = -(-vectors // 32) * 32
+    small = jnp.concatenate([gains, biases], axis=0).astype(narrow)
+    small = jnp.pad(small, ((0, tall - vectors), (0, lanes - own)))
+    images, cotangent = spread(images), spread(cotangent)
+    each, length = images.shape[:2]
+    wide_qkv, wide_small, wide_out, wide_up, wide_down = gather(
+        [w_qkv.astype(narrow), small, w_out.astype(narrow), w_up.astype(narrow), w_down.astype(narrow)],
+        (4, 2, 2, 4, 4),
+        1,
+        depth,
+    )
+    wide_small = (
+        wide_small.reshape(blocks, tall, ways, lanes)[:, :vectors, :, :own]
+        .astype(jnp.float32)
+        .transpose(1, 0, 2, 3)
+        .reshape(vectors, width)
+    )
+    gain, bias = wide_small[: gains.shape[0]], wide_small[gains.shape[0] :]
+    spot = jnp.arange(group, dtype=jnp.int32)
+    live = jnp.concatenate(
+        [lax.rem(me - k + ways, ways) * group + spot for k in range(ways)]
+    ) < PATCH_TOK
+    key_live = live.astype(jnp.float32)
+    rows = images.reshape(each * length, width).astype(jnp.float32)
+    normed_a, inverse_a = normalize(rows)
+    hidden_a = (normed_a * gain[0] + bias[0]).astype(narrow)
+    shift = jnp.concatenate([bias[1], jnp.zeros_like(bias[1]), bias[2]])
+    mixed = (product(hidden_a, wide_qkv) + shift).astype(narrow).reshape(each, length, 3 * width)
+    context = attend_mixed(mixed, key_live).reshape(each * length, width)
+    resid = rows + product(context, wide_out) + bias[3]
+    normed_b, inverse_b = normalize(resid)
+    hidden_b = (normed_b * gain[1] + bias[4]).astype(narrow)
+    pre = product(hidden_b, wide_up) + bias[6:].reshape(-1)
+    active = gelu_value(pre).astype(narrow)
+    out_images = (resid + product(active, wide_down) + bias[5]).astype(narrow)
+    out_images = unspread(out_images.reshape(each, length, width))
+    grad_y = cotangent.astype(jnp.float32) * live[None, :, None].astype(jnp.float32)
+    grad_y = grad_y.reshape(each * length, width)
+    grad_yb = grad_y.astype(narrow)
+    g_down = product(active, grad_yb, TN)
+    grad_pre = product(grad_yb, wide_down, NT) * gelu_slope(pre)
+    grad_preb = grad_pre.astype(narrow)
+    g_up = product(hidden_b, grad_preb, TN)
+    grad_hb = product(grad_preb, wide_up, NT)
+    grad_resid = grad_y + norm_back(grad_hb, normed_b, inverse_b, gain[1])
+    grad_rb = grad_resid.astype(narrow)
+    g_outw = product(context, grad_rb, TN)
+    grad_ctx = product(grad_rb, wide_out, NT).astype(narrow).reshape(each, length, width)
+    grad_mixed, mixed_sum = attend_back_mixed(mixed, grad_ctx, key_live)
+    grad_mixed = grad_mixed.reshape(each * length, 3 * width)
+    g_qkv = product(hidden_a, grad_mixed, TN)
+    grad_ha = product(grad_mixed, wide_qkv, NT)
+    grad_images = (grad_resid + norm_back(grad_ha, normed_a, inverse_a, gain[0])).astype(narrow)
+    grad_images = unspread(grad_images.reshape(each, length, width))
+    g_small = jnp.concatenate(
+        [
+            jnp.stack(
+                [
+                    jnp.sum(grad_ha * normed_a, axis=0),
+                    jnp.sum(grad_hb * normed_b, axis=0),
+                    jnp.sum(grad_ha, axis=0),
+                    mixed_sum[0, :width],
+                    mixed_sum[0, 2 * width :],
+                    jnp.sum(grad_resid, axis=0),
+                    jnp.sum(grad_hb, axis=0),
+                    jnp.sum(grad_y, axis=0),
+                ]
+            ),
+            jnp.sum(grad_pre, axis=0).reshape(-1, width),
+        ],
+        axis=0,
+    )
+    g_small = g_small.reshape(vectors, blocks, ways, own).transpose(1, 0, 2, 3)
+    g_small = jnp.pad(g_small, ((0, 0), (0, tall - vectors), (0, 0), (0, lanes - own)))
+    g_small = g_small.reshape(blocks * tall, ways * lanes)
+    t_down, t_up, t_out, t_qkv, t_small = reduce_sum(
+        [g.astype(narrow) for g in (g_down, g_up, g_outw, g_qkv, g_small)],
+        (4, 4, 2, 4, 2),
+        2,
+        depth,
+    )
+    t_small = t_small[:vectors, :own]
+    totals = (t_qkv, t_out, t_up, t_down, t_small[: gains.shape[0]], t_small[gains.shape[0] :])
+    updated = [
+        adamw(param, grad, first, second)
+        for param, grad, first, second in zip(params, totals, firsts, seconds)
+    ]
+    return (
+        out_images,
+        grad_images,
+        *totals,
+        *(entry[0] for entry in updated),
+        *(entry[1] for entry in updated),
+        *(entry[2] for entry in updated),
+    )
+
+
 def solution(mesh):
+    body = fast_body if is_paired(mesh) else general_body
     return jax.shard_map(
         body,
         mesh=mesh,

time: 717 us -> 495 us (0.69)
  waiting for transfers between devices: 351 us -> 8.09 us
  Pallas kernels: 50.7 us -> 318 us
  local copies, waits for them, and re-layouts: 141 us -> 42.2 us
  other arithmetic: 55.1 us -> 16 us
  between operations: 15.1 us -> 1.68 us
  matrix products: 89.5 us -> 100 us
    pallas_call x2 -> x4, Pallas kernels: 50.7 us -> 318 us  [the longest x1 132 us: reduce_sum(): pl.pallas_call(functools.partial(reduce_kernel, parts, depth, count, shap...]
    all_gather x2 -> x0, waiting for transfers between devices: 141 us -> none  [the longest x1 71.5 us: body(): wide_a = lax.all_gather(part_a, ('seq', 'dp'), axis=0, tiled=True)]
    reduce_scatter x1 -> x0, waiting for transfers between devices: 127 us -> none  [body(): part = lax.psum_scatter(send_a, 'dp', scatter_dimension=0, tiled=True)]
    reshape x7 -> x0, local copies, waits for them, and re-layouts: 56.3 us -> none  [the longest x3 41.8 us: body(): send_a = jnp.concatenate([g_outw.astype(jnp.bfloat16).reshape(blocks, row...]
    transpose x5 -> x0, local copies, waits for them, and re-layouts: 35.8 us -> none  [the longest x2 24.3 us: body(): wide_b[:, :, (1 + fold) * rows_dp:].transpose(1, 2, 0, 3)]
    unnamed x5 -> x0, waiting for transfers between devices: 31.2 us -> none
    concatenate x5 -> x2, other arithmetic: 24.1 us -> 0.62 us  [the longest x1 0.61 us: fast_body(): small = jnp.concatenate([gains, biases], axis=0).astype(narrow)]
    unnamed x141 -> x140, local copies, waits for them, and re-layouts: 32.9 us -> 15 us
  transfers between devices with their start and end apart: 11 -> 4, of which waited for: 10 -> 1; matrix products, arithmetic and copies ran while one was open for 23% -> 10% of each run, Pallas kernels for 7% -> 30%
where the time goes in v1:
time: 495 us; the launch traced here: 490 us
  Pallas kernels  318 us (64%)
  matrix products  100 us (20%)
  local copies, waits for them, and re-layouts  42.2 us (9%)
  other arithmetic  16 us (3%)
  waiting for transfers between devices  8.09 us (2%)
    pallas_call x1, Pallas kernels, reduce_sum(): pl.pallas_call(functools.partial(reduce_kernel, parts, depth, count, shap...  132 us
    pallas_call x1, Pallas kernels, gather(): pl.pallas_call(functools.partial(gather_kernel, parts, depth, len(shards)...  132 us
    dot_general x12, matrix products, product(): return lax.dot_general(a, b, dims, preferred_element_type=jnp.float32)  100 us
    pallas_call x1, Pallas kernels, attend_back_mixed(): pl.pallas_call(attend_back_mixed_kernel, grid=(count, heads), in_specs=sp...  35.9 us
    pallas_call x1, Pallas kernels, attend_mixed(): pl.pallas_call(attend_mixed_kernel, grid=(count, heads), in_specs=specs +...  17.1 us
    unnamed x140, local copies, waits for them, and re-layouts  15 us
    concatenate x10, local copies, waits for them, and re-layouts, fast_body(): jnp.concatenate([jnp.stack([jnp.sum(grad_ha * normed_a, axis=0), jnp.sum(...  13.7 us
  transfers between devices with their start and end apart: 4, of which 1 were waited for; matrix products, arithmetic and copies ran while one was open for 10% of the time, Pallas kernels for 30%

profile of v1, /device:TPU:0, one launch (start us, length us, event | category | flops | bytes accessed | tf_op | source)
XLA Modules:
  0.0 490.1 jit_solution(3364185235577659040)
XLA Ops:
  0.7 2.3 constant_dynamic-slice_fusion.2
  3.0 3.1 collective-permute-start
  6.1 1.4 dynamic-slice_bitcast_fusion.1
  7.5 0.7 convert_element_type.157.refs_3_
  8.3 0.7 convert_element_type.158.refs_4_
  9.0 0.7 convert_element_type.155.refs_0_
  9.7 0.6 convert_element_type.156.refs_2_
  10.4 0.6 fusion.54.refs_1_
  11.0 132.2 %shard_map.395 = (bf16[4,2,2,64,3072]{4,3,2,1,0:T(8,128)(2,1)}, bf16[4,2,2,32,256]{4,3,2,1,0:T(8,128)(2,1)}, bf16[4,2,2,64,1024]{4,3,2,1,0:T(8,128)(2,1)}, bf16[...) custom-call(bf16[64,1536]{1,0:T(8,128)(2,1)} %convert_element_type.155.refs_0_, ...), custom_call_target="tpu_custom_call" | custom-call | tf_op jit(solution)/shard_map/pallas_call | solution.py:309
  143.2 1.0 reshape_reshape.3
  145.1 0.9 copy.57.live_ref
  146.0 0.7 add.285
  147.6 8.0 %fusion.5.q_ref.k_ref.v_ref = bf16[1,592,3072]{2,1,0:T(8,128)(2,1)S(1)} fusion(bf16[1024,3072]{1,0:T(8,128)(2,1)} %bitcast.112, f32[3072]{0:T(1024)S(1)} %pad_maximum_fusion.3, bf16[296,1024]{1,0:T(8,128)(2,1)S(1)} %bitcast.101, bf16[296,1024]{1,0:T(8,128)(2,1)S(1)} %bitcast.96, f32[1024]{0:T(1024)S(1)} %add.263, f32[1024]{0:T(1024)S(1)} %mul.379, ...), kind=kOutput, calls=%fused_computation.12 | convolution fusion | flops 3733635072 | bytes 11166336 | tf_op jit(solution)/shard_map/dot_general | solution.py:824
  155.7 17.1 %shard_map.396 = bf16[1,592,1024]{2,1,0:T(8,128)(2,1)S(1)} custom-call(bf16[1,592,3072]{2,1,0:T(8,128)(2,1)S(1)} %fusion.5.q_ref.k_ref.v_ref, bf16[1,592,3072]{2,1,0:T(8,128)(2,1)S(1)} %fusion.5.q_ref.k_ref.v_ref, bf16[1,592,3072]{2,1,0:T(8,128)(2,1)S(1)} %fusion.5.q_ref.k_ref.v_ref, f32[1,592]{1,0:T(1,128)S(1)} %compare_convert_fusion.1.live_ref), custom_call_target="tpu_custom_call" | custom-call | flops 2871001088 | bytes 3637248 | tf_op jit(solution)/shard_map/pallas_call | solution.py:767
  172.8 1.6 fusion.70
  174.8 11.9 %multiply_convert_fusion = (bf16[592,4096]{1,0:T(8,128)(2,1)}, f32[592,4096]{1,0:T(8,128)}) fusion(f32[4096]{0:T(1024)S(1)} %add.280, bf16[1024,4096]{1,0:T(8,128)(2,1)} %bitcast.110, f32[592,1024]{1,0:T(8,128)S(1)} %get-tuple-element.101, f32[1024]{0:T(1024)S(1)} %add.277, f32[1024]{0:T(1024)S(1)} %mul.387, f32[592]{0:T(1024)S(1)} %add_rsqrt_fusion, ...), kind=kOutput, calls=%fused_computation.6 | convolution fusion | flops 4983635968 | bytes 25391744 | tf_op jit(solution)/shard_map/dot_general | solution.py:824
  186.8 12.9 %fusion.71 = (bf16[4096]{0:T(1024)(128)(2,1)}, bf16[592,4096]{1,0:T(8,128)(2,1)S(1)}) fusion(f32[592,4096]{1,0:T(8,128)} %get-tuple-element.103, f32[4096]{0:T(1024)S(1)} %add.280, bf16[4096,1024]{1,0:T(8,128)(2,1)} %bitcast.108, bf16[1,296,1,1,1,1,1024]{6,1,5,4,3,2,0:T(8,128)(2,1)S(1)} %bitcast.104, ...), kind=kOutput, calls=%fused_computation.143 | convolution fusion | flops 4998787072 | bytes 24176960 | tf_op jit(solution)/shard_map/dot_general | solution.py:824
  199.7 11.3 %multiply_reduce_fusion = (bf16[1024]{0:T(1024)(128)(2,1)}, f32[592]{0:T(1024)S(1)}, f32[592]{0:T(1024)S(1)}, bf16[1024]{0:T(1024)(128)(2,1)}, f32[592,1024]{1,0:T(8,128)S(1)}) fusion(f32[592,1024]{1,0:T(8,128)S(1)} %get-tuple-element.101, f32[592]{0:T(1024)S(1)} %add_rsqrt_fusion, f32[592]{0:T(1024)S(1)} %broadcast_multiply_fusion.4, f32[1024]{0:T(1024)S(1)} %mul.387, ...), kind=kOutput, calls=%fused_computation.33 | convolution fusion | flops 4971508736 | bytes 18105600 | tf_op jit(solution)/shard_map/dot_general | solution.py:824
  211.0 2.9 fusion.66
  214.0 2.5 fusion.29.g_ref
  216.5 3.2 convolution_convert_fusion.3
  219.7 9.6 %convolution_convert_fusion = bf16[1024,4096]{1,0:T(8,128)(2,1)} fusion(bf16[592,4096]{1,0:T(8,128)(2,1)S(1)} %bitcast.117, f32[592,1024]{1,0:T(8,128)S(1)} %get-tuple-element.101, f32[1024]{0:T(1024)S(1)} %copy-done.52, f32[1024]{0:T(1024)S(1)} %copy-done.41, f32[592]{0:T(1024)S(1)} %add_rsqrt_fusion, f32[592]{0:T(1024)S(1)} %broadcast_multiply_fusion.4), kind=kOutput, calls=%fused_computation.8 | convolution fusion | flops 4973281280 | bytes 15676032 | tf_op jit(solution)/shard_map/dot_general | solution.py:824
  229.3 35.9 %shard_map.397 = (bf16[1,592,3072]{2,1,0:T(8,128)(2,1)}, f32[1,3072]{1,0:T(1,128)}) custom-call(bf16[1,592,3072]{2,1,0:T(8,128)(2,1)} %copy-done, bf16[1,592,3072]{2,1,0:T(8,128)(2,1)} %copy-done, bf16[1,592,3072]{2,1,0:T(8,128)(2,1)} %copy-done, bf16[1,592,1024]{2,1,0:T(8,128)(2,1)} %fusion.29.g_ref, f32[592,1]{1,0:T(8,128)} %copy.57.live_ref), custom_call_target="tpu_custom_call" | custom-call | flops 7177502720 | bytes 7274496 | tf_op jit(solution)/shard_map/pallas_call | solution.py:803
  265.2 9.5 %convolution_convert_fusion.2 = bf16[1024,3072]{1,0:T(8,128)(2,1)} fusion(bf16[1,592,3072]{2,1,0:T(8,128)(2,1)} %get-tuple-element.43, bf16[296,1024]{1,0:T(8,128)(2,1)S(1)} %bitcast.102, bf16[296,1024]{1,0:T(8,128)(2,1)S(1)} %bitcast.97, f32[1024]{0:T(1024)S(1)} %copy-done.50, f32[1024]{0:T(1024)S(1)} %copy-done.38, f32[592]{0:T(1024)S(1)} %add_rsqrt_fusion.1, ...), kind=kOutput, calls=%fused_computation.11 | convolution fusion | flops 3733143552 | bytes 11154048 | tf_op jit(solution)/shard_map/dot_general | solution.py:824
  274.7 9.1 %fusion.21 = (bf16[1024]{0:T(1024)(128)(2,1)}, f32[592]{0:T(1024)}, f32[592]{0:T(1024)}, bf16[1024]{0:T(1024)(128)(2,1)}, f32[592,1024]{1,0:T(8,128)}) fusion(f32[592]{0:T(1024)S(1)} %add_rsqrt_fusion.1, f32[592]{0:T(1024)S(1)} %broadcast_multiply_fusion.5, bf16[1,296,1024]{2,1,0:T(8,128)(2,1)S(1)} %copy-done.4, ...), kind=kOutput, calls=%fused_computation.30 | convolution fusion | flops 3732419584 | bytes 13583616 | tf_op jit(solution)/shard_map/dot_general | solution.py:824
  283.8 1.4 concatenate.125
  285.1 1.3 constant_dynamic-update-slice_fusion.8
  286.4 1.4 concatenate.126
  287.8 1.4 concatenate.127
  289.2 0.7 convert.51
  289.9 0.6 slice_reduce_fusion
  290.5 1.4 concatenate.128
  291.8 1.4 concatenate.129
  293.2 1.4 concatenate.130
  294.6 1.4 concatenate.131
  295.9 1.4 concatenate.132
  297.3 1.4 concatenate.133
  298.7 1.3 constant_dynamic-update-slice_fusion.7
  300.0 1.3 constant_dynamic-update-slice_fusion.6
  301.3 1.3 constant_dynamic-update-slice_fusion.5
  302.6 1.3 constant_dynamic-update-slice_fusion.4
  303.9 1.3 constant_dynamic-update-slice_fusion.3
  305.2 1.3 constant_dynamic-update-slice_fusion.2
  306.5 1.3 constant_dynamic-update-slice_fusion.1
  307.8 1.4 constant_dynamic-update-slice_fusion
  309.2 1.8 pad.10
  310.9 1.8 reshape.484
  312.8 1.7 copy.59.refs_4_
  314.5 11.2 %convolution_convert_fusion.1 = bf16[4096,1024]{1,0:T(8,128)(2,1)} fusion(bf16[592,4096]{1,0:T(8,128)(2,1)} %get-tuple-element.102, f32[592]{0:T(1024)} %copy-done.44, bf16[296,1024]{1,0:T(8,128)(2,1)} %bitcast.105, bf16[296,1024]{1,0:T(8,128)(2,1)} %get-tuple-element.85), kind=kOutput, calls=%fused_computation.9 | convolution fusion | flops 4973887488 | bytes 14453056 | tf_op jit(solution)/shard_map/dot_general | solution.py:824
  325.8 132.5 %shard_map.398 = (f32[256,512]{1,0:T(8,128)}, f32[64,2048]{1,0:T(8,128)}, f32[64,512]{1,0:T(8,128)}, f32[64,1536]{1,0:T(8,128)}, f32[32,128]{1,0:T(8,128)}) custom-call(bf16[4,2,2,256,1024]{4,3,2,1,0:T(8,128)(2,1)} %bitcast.99, bf16[4,2,2,64,4096]{4,3,2,1,0:T(8,128)(2,1)} %bitcast.98, bf16[4,2,2,64,1024]{4,3,2,1,0:T(8,128)(2,1)} %bitcast.103, ...), custom_call_target="tpu_custom_call" | custom-call | tf_op jit(solution)/shard_map/pallas_call | solution.py:486
  458.4 1.4 fusion.34
  460.4 1.0 copy-done.2
  461.4 9.5 %fusion.30 = bf16[1,592,1024]{2,1,0:T(8,128)(2,1)S(1)} fusion(f32[592,1024]{1,0:T(8,128)S(1)} %copy-done.2, bf16[592,4096]{1,0:T(8,128)(2,1)} %get-tuple-element.102, bf16[4096,1024]{1,0:T(8,128)(2,1)} %bitcast.109, f32[1024]{0:T(1024)S(1)} %copy-done.48), kind=kOutput, calls=%fused_computation.53 | convolution fusion | flops 4967874560 | bytes 16879616 | tf_op jit(solution)/shard_map/dot_general | solution.py:824
  471.3 0.8 collective-permute-start.1
  472.4 1.4 multiply_subtract_fusion.1
  474.0 1.4 multiply_subtract_fusion
  475.4 0.8 multiply_subtract_fusion.3
  476.2 0.6 multiply_subtract_fusion.4
  477.5 1.2 multiply_subtract_fusion.2
  478.8 8.1 %collective-permute-done.1 = bf16[1,296,1024]{2,1,0:T(8,128)(2,1)S(1)} collective-permute-done((bf16[1,296,1024]{2,1,0:T(8,128)(2,1)S(1)}, bf16[1,296,1024]{2,1,0:T(8,128)(2,1)S(1)}, u32[]{:S(2)}, u32[]{:S(2)}) %collective-permute-start.1) | collective-permute-done | bytes 606240 | tf_op jit(solution)/shard_map/ppermute | solution.py:179
  486.9 0.8 copy.79
  487.7 0.7 copy.80
  488.4 0.8 copy.81
  489.2 0.8 copy.82
  (174 shorter events, 4.4 us)
Async XLA Ops:
  0.7 5.4 %copy-start.18 = (bf16[2,296,1024]{2,1,0:T(8,128)(2,1)S(1)}, bf16[2,296,1024]{2,1,0:T(8,128)(2,1)}, u32[]{:S(2)}) copy-start(bf16[2,296,1024]{2,1,0:T(8,128)(2,1)} %param.21) | copy-start | bytes 3637252
  0.7 6.8 %copy-start.8 = (f32[64,2048]{1,0:T(8,128)S(1)}, f32[64,2048]{1,0:T(8,128)}, u32[]{:S(2)}) copy-start(f32[64,2048]{1,0:T(8,128)} %param.24) | copy-start | bytes 1572868
  3.0 5.3 %copy-start.9 = (f32[256,512]{1,0:T(8,128)S(1)}, f32[256,512]{1,0:T(8,128)}, u32[]{:S(2)}) copy-start(f32[256,512]{1,0:T(8,128)} %param.25) | copy-start | bytes 1572868
  3.0 6.0 %copy-start.13 = (f32[64,1536]{1,0:T(8,128)S(1)}, f32[64,1536]{1,0:T(8,128)}, u32[]{:S(2)}) copy-start(f32[64,1536]{1,0:T(8,128)} %param.22) | copy-start | bytes 1179652
  3.0 6.7 %copy-start.26 = (f32[64,512]{1,0:T(8,128)S(1)}, f32[64,512]{1,0:T(8,128)}, u32[]{:S(2)}) copy-start(f32[64,512]{1,0:T(8,128)} %param.23) | copy-start | bytes 393220
  3.0 7.4 %copy-start.35 = (f32[10,32]{1,0:T(8,128)S(1)}, f32[10,32]{1,0:T(8,128)}, u32[]{:S(2)}) copy-start(f32[10,32]{1,0:T(8,128)} %param.27) | copy-start | bytes 3844
  3.0 7.4 %copy-start.55 = (f32[2,32]{1,0:T(2,128)S(1)}, f32[2,32]{1,0:T(2,128)}, u32[]{:S(2)}) copy-start(f32[2,32]{1,0:T(2,128)} %param.26) | copy-start | bytes 772
  3.0 143.8 %collective-permute-start = (bf16[1,296,1024]{2,1,0:T(8,128)(2,1)}, bf16[1,296,1024]{2,1,0:T(8,128)(2,1)S(1)}, u32[]{:S(2)}, u32[]{:S(2)}) collective-permute-start(bf16[1,296,1024]{2,1,0:T(8,128)(2,1)} %get-tuple-element.91), channel_id=1, source_target_pairs={{0,1},{1,0},{2,3},{3,2},{4,5},{5,4},{6,7},{7,6},{8,9},{9,8},{10,11... | collective-permute-start | bytes 1818632 | tf_op jit(solution)/shard_map/ppermute | solution.py:166
  7.5 179.3 %collective-permute-start.2 = (bf16[1,296,1024]{2,1,0:T(8,128)(2,1)}, bf16[1,296,1024]{2,1,0:T(8,128)(2,1)S(1)}, u32[]{:S(2)}, u32[]{:S(2)}) collective-permute-start(bf16[1,296,1024]{2,1,0:T(8,128)(2,1)} %get-tuple-element.87), channel_id=1, source_target_pairs={{0,1},{1,0},{2,3},{3,2},{4,5},{5,4},{6,7},{7,6},{8,9},{9,8},{10,11... | collective-permute-start | bytes 1818632 | tf_op jit(solution)/shard_map/ppermute | solution.py:166
  144.6 11.1 %copy-start.37 = (f32[1024]{0:T(1024)}, f32[1024]{0:T(1024)S(1)}, u32[]{:S(2)}) copy-start(f32[1024]{0:T(1024)S(1)} %mul.379) | copy-start | bytes 12292
  144.7 11.0 %copy-start.49 = (f32[1024]{0:T(1024)}, f32[1024]{0:T(1024)S(1)}, u32[]{:S(2)}) copy-start(f32[1024]{0:T(1024)S(1)} %add.263) | copy-start | bytes 12292
  144.8 54.8 %copy-start.40 = (f32[1024]{0:T(1024)}, f32[1024]{0:T(1024)S(1)}, u32[]{:S(2)}) copy-start(f32[1024]{0:T(1024)S(1)} %mul.387) | copy-start | bytes 12292
  144.9 29.9 %copy-start.51 = (f32[1024]{0:T(1024)}, f32[1024]{0:T(1024)S(1)}, u32[]{:S(2)}) copy-start(f32[1024]{0:T(1024)S(1)} %add.277) | copy-start | bytes 12292
  146.8 64.2 %copy-start.44 = (f32[592]{0:T(1024)}, f32[592]{0:T(1024)S(1)}, u32[]{:S(2)}) copy-start(f32[592]{0:T(1024)S(1)} %fusion.55) | copy-start | bytes 7108
  146.8 25.9 %copy-start.3 = (bf16[1,296,1024]{2,1,0:T(8,128)(2,1)}, bf16[1,296,1024]{2,1,0:T(8,128)(2,1)S(1)}, u32[]{:S(2)}) copy-start(bf16[1,296,1024]{2,1,0:T(8,128)(2,1)S(1)} %collective-permute-done) | copy-start | bytes 1818628
  147.1 127.6 %copy-start.33 = (f32[592]{0:T(1024)}, f32[592]{0:T(1024)S(1)}, u32[]{:S(2)}) copy-start(f32[592]{0:T(1024)S(1)} %broadcast_multiply_fusion.5) | copy-start | bytes 7108
  147.6 127.1 %copy-start.42 = (f32[592]{0:T(1024)}, f32[592]{0:T(1024)S(1)}, u32[]{:S(2)}) copy-start(f32[592]{0:T(1024)S(1)} %add_rsqrt_fusion.1) | copy-start | bytes 7108
  155.7 17.1 %copy-start = (bf16[1,592,3072]{2,1,0:T(8,128)(2,1)}, bf16[1,592,3072]{2,1,0:T(8,128)(2,1)S(1)}, u32[]{:S(2)}) copy-start(bf16[1,592,3072]{2,1,0:T(8,128)(2,1)S(1)} %fusion.5.q_ref.k_ref.v_ref) | copy-start | bytes 10911748
  155.7 17.1 %copy-start.59 = (bf16[4,2,2,64,1024]{4,3,2,1,0:T(8,128)(2,1)S(1)}, bf16[4,2,2,64,1024]{4,3,2,1,0:T(8,128)(2,1)}, u32[]{:S(2)}) copy-start(bf16[4,2,2,64,1024]{4,3,2,1,0:T(8,128)(2,1)} %get-tuple-element.40) | copy-start | bytes 6291460
  174.4 45.3 %copy-start.1 = (f32[592,1024]{1,0:T(8,128)}, f32[592,1024]{1,0:T(8,128)S(1)}, u32[]{:S(2)}) copy-start(f32[592,1024]{1,0:T(8,128)S(1)} %get-tuple-element.101) | copy-start | bytes 7274500
  174.8 12.0 %copy-start.21 = (bf16[1,296,1,1,1,1,1024]{6,1,5,4,3,2,0:T(8,128)(2,1)S(1)}, bf16[1,296,1,1,1,1,1024]{6,1,5,4,3,2,0:T(8,128)(2,1)}, u32[]{:S(2)}) copy-start(bf16[1,296,1,1,1,1,1024]{6,1,5,4,3,2,0:T(8,128)(2,1)} %get-tuple-element.86) | copy-start | bytes 1818628
  186.7 12.9 %copy-start.19 = (bf16[1,296,1024]{2,1,0:T(8,128)(2,1)}, bf16[1,296,1024]{2,1,0:T(8,128)(2,1)S(1)}, u32[]{:S(2)}) copy-start(bf16[1,296,1024]{2,1,0:T(8,128)(2,1)S(1)} %collective-permute-done.2) | copy-start | bytes 1818628
  199.7 11.3 %copy-start.60 = (bf16[592,4096]{1,0:T(8,128)(2,1)}, bf16[592,4096]{1,0:T(8,128)(2,1)S(1)}, u32[]{:S(2)}) copy-start(bf16[592,4096]{1,0:T(8,128)(2,1)S(1)} %get-tuple-element.107) | copy-start | bytes 14548996
  199.7 11.3 %copy-start.6 = (bf16[296,1024]{1,0:T(8,128)(2,1)S(1)}, bf16[296,1024]{1,0:T(8,128)(2,1)}, u32[]{:S(2)}) copy-start(bf16[296,1024]{1,0:T(8,128)(2,1)} %get-tuple-element.85) | copy-start | bytes 1818628
  199.7 11.4 %copy-start.20 = (bf16[1,296,1024]{2,1,0:T(8,128)(2,1)S(1)}, bf16[1,296,1024]{2,1,0:T(8,128)(2,1)}, u32[]{:S(2)}) copy-start(bf16[1,296,1024]{2,1,0:T(8,128)(2,1)} %copy-done.19) | copy-start | bytes 1818628
  214.0 5.7 %slice-start = ((s8[4849664]{0:T(1024)(128)(4,1)}), s8[655360]{0:T(1024)(128)(4,1)S(1)}, s32[]{:S(2)}) async-start(s8[4849664]{0:T(1024)(128)(4,1)} %bitcast.116), calls=%async_computation | async-start | bytes 1310720
  216.5 3.2 copy-start.41
  216.5 3.2 copy-start.52
  216.5 3.2 slice-start.1
  229.2 35.9 %copy-start.4 = (bf16[1,296,1024]{2,1,0:T(8,128)(2,1)S(1)}, bf16[1,296,1024]{2,1,0:T(8,128)(2,1)}, u32[]{:S(2)}) copy-start(bf16[1,296,1024]{2,1,0:T(8,128)(2,1)} %copy-done.3) | copy-start | bytes 1818628
  229.2 35.9 %copy-start.38 = (f32[1024]{0:T(1024)S(1)}, f32[1024]{0:T(1024)}, u32[]{:S(2)}) copy-start(f32[1024]{0:T(1024)} %copy-done.37) | copy-start | bytes 12292
  229.3 35.9 %copy-start.50 = (f32[1024]{0:T(1024)S(1)}, f32[1024]{0:T(1024)}, u32[]{:S(2)}) copy-start(f32[1024]{0:T(1024)} %copy-done.49) | copy-start | bytes 12292
  265.2 9.5 %copy-start.61 = (bf16[1,592,3072]{2,1,0:T(8,128)(2,1)S(1)}, bf16[1,592,3072]{2,1,0:T(8,128)(2,1)}, u32[]{:S(2)}) copy-start(bf16[1,592,3072]{2,1,0:T(8,128)(2,1)} %get-tuple-element.43) | copy-start | bytes 10911748
  325.7 132.6 %copy-start.54 = (f32[592]{0:T(1024)S(1)}, f32[592]{0:T(1024)}, u32[]{:S(2)}) copy-start(f32[592]{0:T(1024)} %get-tuple-element.53) | copy-start | bytes 7108
  325.7 132.6 %copy-start.53 = (f32[592]{0:T(1024)S(1)}, f32[592]{0:T(1024)}, u32[]{:S(2)}) copy-start(f32[592]{0:T(1024)} %get-tuple-element.54) | copy-start | bytes 7108
  325.7 132.6 %copy-start.5 = (bf16[1,296,1024]{2,1,0:T(8,128)(2,1)S(1)}, bf16[1,296,1024]{2,1,0:T(8,128)(2,1)}, u32[]{:S(2)}) copy-start(bf16[1,296,1024]{2,1,0:T(8,128)(2,1)} %copy-done.3) | copy-start | bytes 1818628
  325.7 132.6 %copy-start.7 = (f32[592,1024]{1,0:T(8,128)S(1)}, f32[592,1024]{1,0:T(8,128)}, u32[]{:S(2)}) copy-start(f32[592,1024]{1,0:T(8,128)} %get-tuple-element.105) | copy-start | bytes 7274500
  325.7 132.6 %copy-start.34 = (f32[592]{0:T(1024)S(1)}, f32[592]{0:T(1024)}, u32[]{:S(2)}) copy-start(f32[592]{0:T(1024)} %copy-done.33) | copy-start | bytes 7108
  325.8 132.6 %copy-start.39 = (f32[1024]{0:T(1024)S(1)}, f32[1024]{0:T(1024)}, u32[]{:S(2)}) copy-start(f32[1024]{0:T(1024)} %copy-done.37) | copy-start | bytes 12292
  325.8 132.6 %copy-start.43 = (f32[592]{0:T(1024)S(1)}, f32[592]{0:T(1024)}, u32[]{:S(2)}) copy-start(f32[592]{0:T(1024)} %copy-done.42) | copy-start | bytes 7108
  459.8 1.7 copy-start.2
  459.8 1.7 copy-start.48
  460.0 18.7 %collective-permute-start.3 = (bf16[1,296,1024]{2,1,0:T(8,128)(2,1)S(1)}, bf16[1,296,1024]{2,1,0:T(8,128)(2,1)S(1)}, u32[]{:S(2)}, u32[]{:S(2)}) collective-permute-start(bf16[1,296,1024]{2,1,0:T(8,128)(2,1)S(1)} %get-tuple-element.83), channel_id=1, source_target_pairs={{0,1},{1,0},{2,3},{3,2},{4,5},{5,4},{6,7},{7,6},{8,9},{9,8},{10,11... | collective-permute-start | bytes 1818632 | tf_op jit(solution)/shard_map/ppermute | solution.py:179
  471.3 2.5 copy-start.10
  471.3 2.5 copy-start.11
  471.3 2.5 copy-start.24
  471.3 2.5 copy-start.25
  471.3 15.5 %collective-permute-start.1 = (bf16[1,296,1024]{2,1,0:T(8,128)(2,1)S(1)}, bf16[1,296,1024]{2,1,0:T(8,128)(2,1)S(1)}, u32[]{:S(2)}, u32[]{:S(2)}) collective-permute-start(bf16[1,296,1024]{2,1,0:T(8,128)(2,1)S(1)} %get-tuple-element.88), channel_id=1, source_target_pairs={{0,1},{1,0},{2,3},{3,2},{4,5},{5,4},{6,7},{7,6},{8,9},{9,8},{10,11... | collective-permute-start | bytes 1818632 | tf_op jit(solution)/shard_map/ppermute | solution.py:179
  473.8 1.6 copy-start.27
  473.8 1.6 copy-start.28
  473.8 1.6 copy-start.31
  473.8 2.4 copy-start.36
  473.9 2.4 copy-start.45
  473.9 2.4 copy-start.46
  473.9 2.4 copy-start.47
  473.9 3.0 copy-start.56
  473.9 3.0 copy-start.57
  473.9 3.0 copy-start.58
  473.9 3.6 copy-start.14
  473.9 3.5 copy-start.15
  473.9 3.5 copy-start.29
  474.0 3.5 copy-start.30
  478.8 11.2 %copy-start.17 = (bf16[2,296,1024]{2,1,0:T(8,128)(2,1)}, bf16[2,296,1024]{2,1,0:T(8,128)(2,1)S(1)}, u32[]{:S(2)}) copy-start(bf16[2,296,1024]{2,1,0:T(8,128)(2,1)S(1)} %constant_dynamic-update-slice_fusion.9) | copy-start | bytes 3637252
  486.9 3.0 copy-start.16
  (4 other events, 5.2 us)

commit v2 on v1

--- a/solution.py
+++ b/solution.py
@@ -752,33 +752,103 @@
     return mesh.shape["seq"] == 2 and mesh.shape["dp"] % 4 == 0
 
 
-def attend_mixed_kernel(q_ref, k_ref, v_ref, live_ref, ctx_ref):
-    attend_kernel(q_ref, k_ref, v_ref, live_ref, ctx_ref)
+def head_lanes(rows):
+    lane = lax.broadcasted_iota(jnp.int32, (rows, LANES), 1)
+    return lane // HEAD_DIM, lax.rem(lane, HEAD_DIM)
+
+
+def three_terms(spot, value):
+    high = value.astype(jnp.bfloat16)
+    rest = value - high.astype(jnp.float32)
+    middle = rest.astype(jnp.bfloat16)
+    low = (rest - middle.astype(jnp.float32)).astype(jnp.bfloat16)
+    zero = jnp.zeros((), jnp.bfloat16)
+    return jnp.where(
+        spot == 0, high, jnp.where(spot == 1, middle, jnp.where(spot == 2, low, zero))
+    )
+
+
+def dead_lane(spot, live):
+    floor = jnp.where(live > 0.5, 0.0, -1e30)
+    ones = jnp.where(spot < 3, 1.0, jnp.where(spot == 3, floor, 0.0))
+    return ones.astype(jnp.bfloat16)
+
+
+def attend_mixed_kernel(q_ref, k_ref, v_ref, live_ref, ctx_ref, lse_ref):
+    q, k, v = q_ref[0], k_ref[0], v_ref[0]
+    half, spot = head_lanes(q.shape[0])
+    q = q * jnp.asarray(HEAD_DIM**-0.5, q.dtype)
+    side_q = (spot == 3).astype(jnp.float32).astype(jnp.bfloat16)
+    side_k = dead_lane(spot, live_ref[...])
+    total = jnp.zeros(q.shape, jnp.float32)
+    lse = jnp.zeros(q.shape, jnp.float32)
+    for h in range(LANES // HEAD_DIM):
+        mask = half == h
+        scores = dot(jnp.where(mask, q, side_q), jnp.where(mask, k, side_k), NT)
+        top = jnp.max(scores, axis=-1, keepdims=True)
+        weights = jnp.exp(scores - top)
+        denom = jnp.sum(weights, axis=-1, keepdims=True)
+        total = jnp.where(mask, dot(weights.astype(jnp.bfloat16), v, NN) * (1.0 / denom), total)
+        lse = jnp.where(mask, lse, top + jnp.log(denom))
+    ctx_ref[0] = total.astype(jnp.bfloat16)
+    lse_ref[0] = lse
+
+
+def mixed_specs(rows, heads):
+    return [
+        pl.BlockSpec((1, rows, LANES), lambda i, h, k=k: (i, 0, h + k * heads)) for k in range(3)
+    ]
 
 
 def attend_mixed(mixed, live):
     count, rows, triple = mixed.shape
     width = triple // 3
     heads = width // LANES
-    specs = [
-        pl.BlockSpec((1, rows, LANES), lambda i, h, k=k: (i, 0, h + k * heads)) for k in range(3)
-    ]
+    specs = mixed_specs(rows, heads)
     pairs = count * rows * rows * width
     return pl.pallas_call(
         attend_mixed_kernel,
         grid=(count, heads),
-        in_specs=specs + [pl.BlockSpec((1, rows), lambda i, h: (0, 0))],
-        out_specs=specs[0],
-        out_shape=jax.ShapeDtypeStruct((count, rows, width), jnp.bfloat16),
+        in_specs=specs + [pl.BlockSpec((rows, 1), lambda i, h: (0, 0))],
+        out_specs=[specs[0], specs[0]],
+        out_shape=[
+            jax.ShapeDtypeStruct((count, rows, width), jnp.bfloat16),
+            jax.ShapeDtypeStruct((count, rows, width), jnp.float32),
+        ],
         cost_estimate=pl.CostEstimate(
             flops=8 * pairs, bytes_accessed=2 * mixed.size, transcendentals=pairs // HEAD_DIM
         ),
         compiler_params=pltpu.CompilerParams(vmem_limit_bytes=48 * 1024 * 1024),
-    )(mixed, mixed, mixed, live.reshape(1, rows))
-
-
-def attend_back_mixed_kernel(q_ref, k_ref, v_ref, g_ref, live_ref, dm_ref, sum_ref, dq, dk, dv):
-    attend_back_kernel(q_ref, k_ref, v_ref, g_ref, live_ref, dq, dk, dv)
+    )(mixed, mixed, mixed, live.reshape(rows, 1))
+
+
+def attend_back_mixed_kernel(
+    q_ref, k_ref, v_ref, g_ref, ctx_ref, lse_ref, live_ref, dm_ref, sum_ref
+):
+    q, k, v, g = q_ref[0], k_ref[0], v_ref[0], g_ref[0]
+    scale = HEAD_DIM**-0.5
+    half, spot = head_lanes(q.shape[0])
+    q = q * jnp.asarray(scale, q.dtype)
+    one = (spot == 3).astype(jnp.float32).astype(jnp.bfloat16)
+    side_q = three_terms(spot, -lse_ref[0]) + one
+    side_k = dead_lane(spot, live_ref[...])
+    side_v = (spot < 3).astype(jnp.float32).astype(jnp.bfloat16)
+    agree = g.astype(jnp.float32) * ctx_ref[0].astype(jnp.float32)
+    dq = jnp.zeros(q.shape, jnp.float32)
+    dk = jnp.zeros(q.shape, jnp.float32)
+    dv = jnp.zeros(q.shape, jnp.float32)
+    for h in range(LANES // HEAD_DIM):
+        mask = half == h
+        delta = jnp.sum(jnp.where(mask, agree, 0.0), axis=1, keepdims=True)
+        q_h = jnp.where(mask, q, side_q)
+        k_h = jnp.where(mask, k, side_k)
+        v_h = jnp.where(mask, v, side_v)
+        g_h = jnp.where(mask, g, three_terms(spot, jnp.broadcast_to(-delta, q.shape)))
+        probs = jnp.exp(dot(k_h, q_h, NT))
+        grad_scores = (probs * dot(v_h, g_h, NT)).astype(jnp.bfloat16)
+        dv = jnp.where(mask, dot(probs.astype(jnp.bfloat16), g, NN), dv)
+        dk = jnp.where(mask, dot(grad_scores, q, NN), dk)
+        dq = jnp.where(mask, dot(grad_scores, k, TN), dq)
     image, head = pl.program_id(0), pl.program_id(1)
     width = dm_ref.shape[2] // 3
 
@@ -786,24 +856,22 @@
     def _():
         sum_ref[...] = jnp.zeros_like(sum_ref)
 
-    for k, part in enumerate((dq, dk, dv)):
-        where = pl.ds(pl.multiple_of(k * width + head * LANES, LANES), LANES)
-        dm_ref[0, :, where] = part[0].astype(jnp.bfloat16)
-        sum_ref[:, where] += jnp.sum(part[0], axis=0, keepdims=True)
-
-
-def attend_back_mixed(mixed, grad_ctx, live):
+    for n, part in enumerate((dq * scale, dk, dv)):
+        where = pl.ds(pl.multiple_of(n * width + head * LANES, LANES), LANES)
+        dm_ref[0, :, where] = part.astype(jnp.bfloat16)
+        sum_ref[:, where] += jnp.sum(part, axis=0, keepdims=True)
+
+
+def attend_back_mixed(mixed, grad_ctx, context, lse, live):
     count, rows, triple = mixed.shape
     width = triple // 3
     heads = width // LANES
-    specs = [
-        pl.BlockSpec((1, rows, LANES), lambda i, h, k=k: (i, 0, h + k * heads)) for k in range(3)
-    ]
+    specs = mixed_specs(rows, heads)
     pairs = count * rows * rows * width
     return pl.pallas_call(
         attend_back_mixed_kernel,
         grid=(count, heads),
-        in_specs=specs + [specs[0], pl.BlockSpec((rows, 1), lambda i, h: (0, 0))],
+        in_specs=specs + [specs[0]] * 3 + [pl.BlockSpec((rows, 1), lambda i, h: (0, 0))],
         out_specs=[
             pl.BlockSpec((1, rows, triple), lambda i, h: (i, 0, 0)),
             pl.BlockSpec((1, triple), lambda i, h: (0, 0)),
@@ -812,16 +880,44 @@
             jax.ShapeDtypeStruct(mixed.shape, jnp.bfloat16),
             jax.ShapeDtypeStruct((1, triple), jnp.float32),
         ],
-        scratch_shapes=[pltpu.VMEM((1, rows, LANES), jnp.float32)] * 3,
         cost_estimate=pl.CostEstimate(
             flops=20 * pairs, bytes_accessed=4 * mixed.size, transcendentals=pairs // HEAD_DIM
         ),
         compiler_params=pltpu.CompilerParams(vmem_limit_bytes=56 * 1024 * 1024),
-    )(mixed, mixed, mixed, grad_ctx, live.reshape(rows, 1))
+    )(mixed, mixed, mixed, grad_ctx, context, lse, live.reshape(rows, 1))
+
+
+def small_kernel(slots, own, lanes, *refs):
+    rows, out_ref, stack = refs[:-2], refs[-2], refs[-1]
+    stack[...] = jnp.zeros_like(stack)
+    out_ref[...] = jnp.zeros_like(out_ref)
+    width = stack.shape[1]
+    at = 0
+    for ref in rows:
+        for start in range(0, ref.shape[1], width):
+            stack[at : at + 1] = ref[:, start : start + width]
+            at += 1
+    filled = stack[...].astype(jnp.bfloat16)
+    for slot in range(slots):
+        piece = filled[:, slot * own : (slot + 1) * own]
+        out_ref[slot // 2, :, (slot % 2) * lanes : (slot % 2) * lanes + own] = piece
+
+
+def pack_small(rows, blocks, tall, own, lanes):
+    width = rows[0].shape[1]
+    return pl.pallas_call(
+        functools.partial(small_kernel, 2 * blocks, own, lanes),
+        out_shape=jax.ShapeDtypeStruct((blocks, tall, 2 * lanes), jnp.bfloat16),
+        scratch_shapes=[pltpu.VMEM((tall, width), jnp.float32)],
+    )(*rows).reshape(blocks * tall, 2 * lanes)
 
 
 def product(a, b, dims=NN):
     return lax.dot_general(a, b, dims, preferred_element_type=jnp.float32)
+
+
+def sum_rows(rows):
+    return jnp.sum(rows, axis=0, keepdims=True)
 
 
 def fast_body(images, cotangent, *rest):
@@ -864,17 +960,19 @@
     hidden_a = (normed_a * gain[0] + bias[0]).astype(narrow)
     shift = jnp.concatenate([bias[1], jnp.zeros_like(bias[1]), bias[2]])
     mixed = (product(hidden_a, wide_qkv) + shift).astype(narrow).reshape(each, length, 3 * width)
-    context = attend_mixed(mixed, key_live).reshape(each * length, width)
+    context, lse = attend_mixed(mixed, key_live)
+    context = context.reshape(each * length, width)
     resid = rows + product(context, wide_out) + bias[3]
     normed_b, inverse_b = normalize(resid)
     hidden_b = (normed_b * gain[1] + bias[4]).astype(narrow)
     pre = product(hidden_b, wide_up) + bias[6:].reshape(-1)
     active = gelu_value(pre).astype(narrow)
     out_images = (resid + product(active, wide_down) + bias[5]).astype(narrow)
-    out_images = unspread(out_images.reshape(each, length, width))
     grad_y = cotangent.astype(jnp.float32) * live[None, :, None].astype(jnp.float32)
     grad_y = grad_y.reshape(each * length, width)
     grad_yb = grad_y.astype(narrow)
+    grad_yb, out_images = lax.optimization_barrier((grad_yb, out_images))
+    out_images = unspread(out_images.reshape(each, length, width))
     g_down = product(active, grad_yb, TN)
     grad_pre = product(grad_yb, wide_down, NT) * gelu_slope(pre)
     grad_preb = grad_pre.astype(narrow)
@@ -884,33 +982,31 @@
     grad_rb = grad_resid.astype(narrow)
     g_outw = product(context, grad_rb, TN)
     grad_ctx = product(grad_rb, wide_out, NT).astype(narrow).reshape(each, length, width)
-    grad_mixed, mixed_sum = attend_back_mixed(mixed, grad_ctx, key_live)
+    grad_mixed, mixed_sum = attend_back_mixed(
+        mixed, grad_ctx, context.reshape(each, length, width), lse, key_live
+    )
     grad_mixed = grad_mixed.reshape(each * length, 3 * width)
     g_qkv = product(hidden_a, grad_mixed, TN)
     grad_ha = product(grad_mixed, wide_qkv, NT)
     grad_images = (grad_resid + norm_back(grad_ha, normed_a, inverse_a, gain[0])).astype(narrow)
     grad_images = unspread(grad_images.reshape(each, length, width))
-    g_small = jnp.concatenate(
+    g_small = pack_small(
         [
-            jnp.stack(
-                [
-                    jnp.sum(grad_ha * normed_a, axis=0),
-                    jnp.sum(grad_hb * normed_b, axis=0),
-                    jnp.sum(grad_ha, axis=0),
-                    mixed_sum[0, :width],
-                    mixed_sum[0, 2 * width :],
-                    jnp.sum(grad_resid, axis=0),
-                    jnp.sum(grad_hb, axis=0),
-                    jnp.sum(grad_y, axis=0),
-                ]
-            ),
-            jnp.sum(grad_pre, axis=0).reshape(-1, width),
+            sum_rows(grad_ha * normed_a),
+            sum_rows(grad_hb * normed_b),
+            sum_rows(grad_ha),
+            mixed_sum[:, :width],
+            mixed_sum[:, 2 * width :],
+            sum_rows(grad_resid),
+            sum_rows(grad_hb),
+            sum_rows(grad_y),
+            sum_rows(grad_pre),
         ],
-        axis=0,
-    )
-    g_small = g_small.reshape(vectors, blocks, ways, own).transpose(1, 0, 2, 3)
-    g_small = jnp.pad(g_small, ((0, 0), (0, tall - vectors), (0, 0), (0, lanes - own)))
-    g_small = g_small.reshape(blocks * tall, ways * lanes)
+        blocks,
+        tall,
+        own,
+        lanes,
+    )
     t_down, t_up, t_out, t_qkv, t_small = reduce_sum(
         [g.astype(narrow) for g in (g_down, g_up, g_outw, g_qkv, g_small)],
         (4, 4, 2, 4, 2),

time: 495 us -> 446 us (0.901)
  local copies, waits for them, and re-layouts: 42.2 us -> 13.1 us
  Pallas kernels: 318 us -> 309 us
  waiting for transfers between devices: 8.09 us -> 0.01 us
  matrix products: 100 us -> 94.9 us
    concatenate x10 -> x0, local copies, waits for them, and re-layouts: 13.7 us -> none  [fast_body(): jnp.concatenate([jnp.stack([jnp.sum(grad_ha * normed_a, axis=0), jnp.sum(...]
    unnamed x140 -> x90, local copies, waits for them, and re-layouts: 15 us -> 3.43 us
    pallas_call x1, Pallas kernels: 35.9 us -> 27.4 us  [attend_back_mixed(): pl.pallas_call(attend_back_mixed_kernel, grid=(count, heads), in_specs=sp...]
    ppermute x2, waiting for transfers between devices: 8.09 us -> 0.01 us  [unspread(): piece = lax.ppermute(piece, 'seq', shift_by(-step, ways))]
    dot_general x12, matrix products: 100 us -> 94.9 us  [product(): return lax.dot_general(a, b, dims, preferred_element_type=jnp.float32)]
  transfers between devices with their start and end apart: 4 -> 4, of which waited for: 1 -> 0; matrix products, arithmetic and copies ran while one was open for 10% -> 12% of each run, Pallas kernels for 30% -> 70%
where the time goes in v2:
time: 446 us; the launch traced here: 443 us
  Pallas kernels  309 us (69%)
  matrix products  94.9 us (21%)
  other arithmetic  19.2 us (4%)
  local copies, waits for them, and re-layouts  13.1 us (3%)
  starting transfers between devices  5.05 us (1%)
    pallas_call x1, Pallas kernels, gather(): pl.pallas_call(functools.partial(gather_kernel, parts, depth, len(shards)...  132 us
    pallas_call x1, Pallas kernels, reduce_sum(): pl.pallas_call(functools.partial(reduce_kernel, parts, depth, count, shap...  132 us
    dot_general x12, matrix products, product(): return lax.dot_general(a, b, dims, preferred_element_type=jnp.float32)  94.9 us
    pallas_call x1, Pallas kernels, attend_back_mixed(): pl.pallas_call(attend_back_mixed_kernel, grid=(count, heads), in_specs=sp...  27.4 us
    pallas_call x1, Pallas kernels, attend_mixed(): pl.pallas_call(attend_mixed_kernel, grid=(count, heads), in_specs=specs +...  16 us
  transfers between devices with their start and end apart: 4, of which 0 were waited for; matrix products, arithmetic and copies ran while one was open for 12% of the time, Pallas kernels for 70%

profile of v2, /device:TPU:0, one launch (start us, length us, event | category | flops | bytes accessed | tf_op | source)
XLA Modules:
  0.0 442.8 jit_solution(15780328285396773698)
XLA Ops:
  0.7 2.3 dynamic-slice_bitcast_fusion
  3.0 3.0 collective-permute-start
  6.0 0.9 constant_dynamic-slice_fusion.1
  6.9 1.7 convert_element_type.110.refs_0_
  8.7 1.5 convert_element_type.111.refs_2_
  10.2 0.7 convert_element_type.112.refs_3_
  10.9 0.7 convert_element_type.113.refs_4_
  11.7 0.6 fusion.45.refs_1_
  12.3 132.2 %shard_map.395 = (bf16[4,2,2,64,3072]{4,3,2,1,0:T(8,128)(2,1)}, bf16[4,2,2,32,256]{4,3,2,1,0:T(8,128)(2,1)}, bf16[4,2,2,64,1024]{4,3,2,1,0:T(8,128)(2,1)}, bf16[...) custom-call(bf16[64,1536]{1,0:T(8,128)(2,1)} %convert_element_type.110.refs_0_, ...), custom_call_target="tpu_custom_call" | custom-call | tf_op jit(solution)/shard_map/pallas_call | solution.py:309
  144.5 1.0 reshape_reshape.6
  145.5 0.1 convert_bitcast_fusion.1
  145.6 0.1 add.259
  145.7 0.1 squeeze.7
  145.8 0.1 squeeze.6
  145.9 0.1 add.253
  146.0 0.1 mul.366
  146.1 0.1 add_compare_fusion.1
  146.1 0.2 copy.53
  146.4 0.1 add.266
  146.5 0.1 add.263
  146.6 0.1 mul.372
  146.7 0.1 add.271
  146.8 0.1 fusion.46
  146.9 0.2 convert_reduce_fusion
  147.1 0.5 fusion.22
  147.6 9.5 %fusion.5.q_ref.k_ref.v_ref = bf16[1,592,3072]{2,1,0:T(8,128)(2,1)} fusion(bf16[1024,3072]{1,0:T(8,128)(2,1)} %bitcast.121, f32[3072]{0:T(1024)S(1)} %pad_maximum_fusion.2, bf16[296,1024]{1,0:T(8,128)(2,1)S(1)} %bitcast.99, bf16[296,1024]{1,0:T(8,128)(2,1)S(1)} %bitcast.94, f32[1024]{0:T(1024)S(1)} %add.253, f32[1024]{0:T(1024)S(1)} %mul.366, ...), kind=kOutput, calls=%fused_computation.12 | convolution fusion | flops 3733635072 | bytes 11166336 | tf_op jit(solution)/shard_map/dot_general | solution.py:916
  157.1 16.0 %shard_map.396 = (bf16[1,592,1024]{2,1,0:T(8,128)(2,1)S(1)}, f32[1,592,1024]{2,1,0:T(8,128)S(1)}) custom-call(bf16[1,592,3072]{2,1,0:T(8,128)(2,1)} %fusion.5.q_ref.k_ref.v_ref, bf16[1,592,3072]{2,1,0:T(8,128)(2,1)} %fusion.5.q_ref.k_ref.v_ref, bf16[1,592,3072]{2,1,0:T(8,128)(2,1)} %fusion.5.q_ref.k_ref.v_ref, f32[592,1]{1,0:T(8,128)S(1)} %convert_element_type.116.live_ref), custom_call_target="tpu_custom_call" | custom-call | flops 2871001088 | bytes 3637248 | tf_op jit(solution)/shard_map/pallas_call | solution.py:809
  173.2 4.5 %fusion.60 = (f32[592]{0:T(1024)S(1)}, f32[592,1024]{1,0:T(8,128)S(1)}) fusion(f32[1024]{0:T(1024)S(1)} %add.259, bf16[1024,1024]{1,0:T(8,128)(2,1)} %bitcast.123, bf16[1,592,1024]{2,1,0:T(8,128)(2,1)S(1)} %get-tuple-element.44.ctx_ref, bf16[1,296,1024]{2,1,0:T(8,128)(2,1)S(1)} %collective-permute-done.1, bf16[1,296,1024]{2,1,0:T(8,128)(2,1)S(1)} %get-tuple-element.93), kind=kOutput, calls=%fused_computation.120 | convolution fusion | flops 1245756800 | bytes 6953280 | tf_op jit(solution)/shard_map/dot_general | solution.py:916
  177.6 0.4 multiply_reduce_fusion.2
  178.1 0.3 fusion.28
  178.3 0.2 slice-done.1
  178.5 10.2 %multiply_convert_fusion = (bf16[592,4096]{1,0:T(8,128)(2,1)}, f32[592,4096]{1,0:T(8,128)}) fusion(f32[4096]{0:T(1024)S(1)} %add.266, bf16[1024,4096]{1,0:T(8,128)(2,1)S(1)} %bitcast.116, f32[592,1024]{1,0:T(8,128)S(1)} %get-tuple-element.108, f32[1024]{0:T(1024)S(1)} %add.263, f32[1024]{0:T(1024)S(1)} %mul.372, f32[592]{0:T(1024)S(1)} %add_rsqrt_fusion, ...), kind=kOutput, calls=%fused_computation.6 | convolution fusion | flops 4983635968 | bytes 25391744 | tf_op jit(solution)/shard_map/dot_general | solution.py:916
  188.8 7.6 %add_convert_fusion.1 = bf16[592,1024]{1,0:T(8,128)(2,1)S(1)} fusion(f32[592,1024]{1,0:T(8,128)S(1)} %get-tuple-element.108, bf16[592,4096]{1,0:T(8,128)(2,1)} %get-tuple-element.109, bf16[4096,1024]{1,0:T(8,128)(2,1)S(1)} %bitcast.120, f32[1024]{0:T(1024)S(1)} %add.271), kind=kOutput, calls=%fused_computation.39 | convolution fusion | flops 4967874560 | bytes 16879616 | tf_op jit(solution)/shard_map/dot_general | solution.py:916
  196.3 9.1 %convolution_convert_fusion.1 = bf16[4096,1024]{1,0:T(8,128)(2,1)} fusion(bf16[592,4096]{1,0:T(8,128)(2,1)S(1)} %copy-done.38, bf16[592,1024]{1,0:T(8,128)(2,1)S(1)} %fusion.28), kind=kOutput, calls=%fused_computation.9 | convolution fusion | flops 4970250240 | bytes 14450688 | tf_op jit(solution)/shard_map/dot_general | solution.py:916
  205.5 12.6 %fusion.61 = (f32[4096]{0:T(1024)}, bf16[592,4096]{1,0:T(8,128)(2,1)S(1)}) fusion(f32[592,4096]{1,0:T(8,128)} %get-tuple-element.110, f32[4096]{0:T(1024)S(1)} %add.266, bf16[592,1024]{1,0:T(8,128)(2,1)S(1)} %fusion.28, bf16[4096,1024]{1,0:T(8,128)(2,1)} %bitcast.117), kind=kOutput, calls=%fused_computation.121 | convolution fusion | flops 4995149824 | bytes 24182784 | tf_op jit(solution)/shard_map/dot_general | solution.py:916
  218.1 9.0 %multiply_reduce_fusion = (f32[1024]{0:T(1024)}, f32[592]{0:T(1024)S(1)}, f32[592]{0:T(1024)S(1)}, f32[1024]{0:T(1024)}, f32[592,1024]{1,0:T(8,128)S(1)}) fusion(f32[592,1024]{1,0:T(8,128)S(1)} %get-tuple-element.108, f32[592]{0:T(1024)S(1)} %add_rsqrt_fusion, f32[592]{0:T(1024)S(1)} %broadcast_multiply_fusion.4, f32[1024]{0:T(1024)S(1)} %mul.372, ...), kind=kOutput, calls=%fused_computation.33 | convolution fusion | flops 4971508736 | bytes 18109696 | tf_op jit(solution)/shard_map/dot_general | solution.py:916
  227.1 9.7 %convolution_convert_fusion = bf16[1024,4096]{1,0:T(8,128)(2,1)} fusion(bf16[592,4096]{1,0:T(8,128)(2,1)S(1)} %get-tuple-element.114, f32[592,1024]{1,0:T(8,128)S(1)} %get-tuple-element.108, f32[1024]{0:T(1024)S(1)} %add.263, f32[1024]{0:T(1024)S(1)} %mul.372, f32[592]{0:T(1024)S(1)} %add_rsqrt_fusion, f32[592]{0:T(1024)S(1)} %broadcast_multiply_fusion.4), kind=kOutput, calls=%fused_computation.8 | convolution fusion | flops 4973281280 | bytes 15676032 | tf_op jit(solution)/shard_map/dot_general | solution.py:916
  236.8 2.3 fusion.55
  239.1 2.5 fusion.29.g_ref
  241.6 3.3 convolution_convert_fusion.3
  244.8 0.1 broadcast.196.clone
  245.0 1.0 fusion.57
  246.0 0.5 collective-permute-start.2
  246.5 27.4 %shard_map.397 = (bf16[1,592,3072]{2,1,0:T(8,128)(2,1)}, f32[1,3072]{1,0:T(1,128)}) custom-call(bf16[1,592,3072]{2,1,0:T(8,128)(2,1)} %fusion.5.q_ref.k_ref.v_ref, bf16[1,592,3072]{2,1,0:T(8,128)(2,1)} %fusion.5.q_ref.k_ref.v_ref, bf16[1,592,3072]{2,1,0:T(8,128)(2,1)} %fusion.5.q_ref.k_ref.v_ref, bf16[1,592,1024]{2,1,0:T(8,128)(2,1)} %fusion.29.g_ref, ...), custom_call_target="tpu_custom_call" | custom-call | flops 7177502720 | bytes 7274496 | tf_op jit(solution)/shard_map/pallas_call | solution.py:871
  273.9 9.7 %convolution_convert_fusion.2 = bf16[1024,3072]{1,0:T(8,128)(2,1)} fusion(bf16[1,592,3072]{2,1,0:T(8,128)(2,1)} %get-tuple-element.51, bf16[296,1024]{1,0:T(8,128)(2,1)S(1)} %bitcast.100, bf16[296,1024]{1,0:T(8,128)(2,1)S(1)} %bitcast.95, f32[1024]{0:T(1024)S(1)} %copy-done.31, f32[1024]{0:T(1024)S(1)} %copy-done.26, f32[592]{0:T(1024)S(1)} %add_rsqrt_fusion.1, ...), kind=kOutput, calls=%fused_computation.11 | convolution fusion | flops 3733143552 | bytes 11154048 | tf_op jit(solution)/shard_map/dot_general | solution.py:916
  283.6 7.3 %fusion.21 = (f32[1024]{0:T(1024)}, f32[592]{0:T(1024)S(1)}, f32[592]{0:T(1024)S(1)}, f32[1024]{0:T(1024)}, f32[592,1024]{1,0:T(8,128)S(1)}) fusion(f32[592]{0:T(1024)S(1)} %add_rsqrt_fusion.1, f32[592]{0:T(1024)S(1)} %broadcast_multiply_fusion.5, bf16[1,296,1024]{2,1,0:T(8,128)(2,1)S(1)} %collective-permute-done.1, ...), kind=kOutput, calls=%fused_computation.30 | convolution fusion | flops 3732419584 | bytes 13587712 | tf_op jit(solution)/shard_map/dot_general | solution.py:916
  290.9 1.4 fusion.30
  292.3 0.1 broadcast.196.clone.1
  292.4 0.9 fusion.56
  293.3 1.5 collective-permute-start.3
  294.9 0.6 fusion.59
  295.5 1.7 shard_map.398
  297.2 131.8 %shard_map.399 = (f32[256,512]{1,0:T(8,128)}, f32[64,2048]{1,0:T(8,128)}, f32[64,512]{1,0:T(8,128)}, f32[64,1536]{1,0:T(8,128)}, f32[32,128]{1,0:T(8,128)}) custom-call(bf16[4,2,2,256,1024]{4,3,2,1,0:T(8,128)(2,1)} %bitcast.96, bf16[4,2,2,64,4096]{4,3,2,1,0:T(8,128)(2,1)} %bitcast.97, bf16[4,2,2,64,1024]{4,3,2,1,0:T(8,128)(2,1)} %bitcast.103, ...), custom_call_target="tpu_custom_call" | custom-call | tf_op jit(solution)/shard_map/pallas_call | solution.py:486
  429.1 1.5 multiply_subtract_fusion.4
  430.6 2.2 multiply_subtract_fusion.2
  432.9 0.8 multiply_subtract_fusion.3
  433.7 1.4 multiply_subtract_fusion
  435.2 1.3 multiply_subtract_fusion.5
  436.5 1.4 multiply_subtract_fusion.1
  438.0 1.5 constant_dynamic-update-slice_fusion
  439.5 0.8 copy.64
  440.3 0.7 copy.65
  441.0 0.8 copy.66
  441.8 0.8 copy.67
  (111 shorter events, 0.4 us)
Async XLA Ops:
  0.7 5.3 %copy-start.10 = (bf16[2,296,1024]{2,1,0:T(8,128)(2,1)S(1)}, bf16[2,296,1024]{2,1,0:T(8,128)(2,1)}, u32[]{:S(2)}) copy-start(bf16[2,296,1024]{2,1,0:T(8,128)(2,1)} %param.20) | copy-start | bytes 3637252
  0.7 7.9 %copy-start.23 = (f32[10,32]{1,0:T(8,128)S(1)}, f32[10,32]{1,0:T(8,128)}, u32[]{:S(2)}) copy-start(f32[10,32]{1,0:T(8,128)} %param.27) | copy-start | bytes 3844
  0.7 7.9 %copy-start.32 = (f32[2,32]{1,0:T(2,128)S(1)}, f32[2,32]{1,0:T(2,128)}, u32[]{:S(2)}) copy-start(f32[2,32]{1,0:T(2,128)} %param.26) | copy-start | bytes 772
  0.7 9.5 %copy-start.4 = (f32[64,2048]{1,0:T(8,128)S(1)}, f32[64,2048]{1,0:T(8,128)}, u32[]{:S(2)}) copy-start(f32[64,2048]{1,0:T(8,128)} %param.24) | copy-start | bytes 1572868
  3.0 7.9 %copy-start.3 = (f32[256,512]{1,0:T(8,128)S(1)}, f32[256,512]{1,0:T(8,128)}, u32[]{:S(2)}) copy-start(f32[256,512]{1,0:T(8,128)} %param.25) | copy-start | bytes 1572868
  3.0 175.0 %collective-permute-start = (bf16[1,296,1024]{2,1,0:T(8,128)(2,1)}, bf16[1,296,1024]{2,1,0:T(8,128)(2,1)S(1)}, u32[]{:S(2)}, u32[]{:S(2)}) collective-permute-start(bf16[1,296,1024]{2,1,0:T(8,128)(2,1)} %get-tuple-element.96), channel_id=1, source_target_pairs={{0,1},{1,0},{2,3},{3,2},{4,5},{5,4},{6,7},{7,6},{8,9},{9,8},{10,11... | collective-permute-start | bytes 1818632 | tf_op jit(solution)/shard_map/ppermute | solution.py:166
  6.9 139.9 %collective-permute-start.1 = (bf16[1,296,1024]{2,1,0:T(8,128)(2,1)}, bf16[1,296,1024]{2,1,0:T(8,128)(2,1)S(1)}, u32[]{:S(2)}, u32[]{:S(2)}) collective-permute-start(bf16[1,296,1024]{2,1,0:T(8,128)(2,1)} %get-tuple-element.94), channel_id=1, source_target_pairs={{0,1},{1,0},{2,3},{3,2},{4,5},{5,4},{6,7},{7,6},{8,9},{9,8},{10,11... | collective-permute-start | bytes 1818632 | tf_op jit(solution)/shard_map/ppermute | solution.py:166
  146.0 11.2 %copy-start.30 = (f32[1024]{0:T(1024)}, f32[1024]{0:T(1024)S(1)}, u32[]{:S(2)}) copy-start(f32[1024]{0:T(1024)S(1)} %add.253) | copy-start | bytes 12292
  146.0 11.1 %copy-start.25 = (f32[1024]{0:T(1024)}, f32[1024]{0:T(1024)S(1)}, u32[]{:S(2)}) copy-start(f32[1024]{0:T(1024)S(1)} %mul.366) | copy-start | bytes 12292
  146.4 10.7 %copy-start = (f32[592,1]{1,0:T(8,128)}, f32[592,1]{1,0:T(8,128)S(1)}, u32[]{:S(2)}) copy-start(f32[592,1]{1,0:T(8,128)S(1)} %convert_element_type.116.live_ref) | copy-start | bytes 7108
  173.1 4.5 %copy-start.1 = (f32[1,592,1024]{2,1,0:T(8,128)}, f32[1,592,1024]{2,1,0:T(8,128)S(1)}, u32[]{:S(2)}) copy-start(f32[1,592,1024]{2,1,0:T(8,128)S(1)} %get-tuple-element.50.lse_ref) | copy-start | bytes 7274500
  173.1 68.4 %copy-start.2 = (bf16[1,592,1024]{2,1,0:T(8,128)(2,1)}, bf16[1,592,1024]{2,1,0:T(8,128)(2,1)S(1)}, u32[]{:S(2)}) copy-start(bf16[1,592,1024]{2,1,0:T(8,128)(2,1)S(1)} %get-tuple-element.44.ctx_ref) | copy-start | bytes 3637252
  173.1 5.2 %slice-start = ((s8[8388608]{0:T(1024)(128)(4,1)}), s8[4194304]{0:T(1024)(128)(4,1)S(1)}, s32[]{:S(2)}) async-start(s8[8388608]{0:T(1024)(128)(4,1)} %bitcast.114), calls=%async_computation | async-start | bytes 8388608
  173.2 5.4 %slice-start.1 = ((s8[8388608]{0:T(1024)(128)(4,1)}), s8[4194304]{0:T(1024)(128)(4,1)S(1)}, s32[]{:S(2)}) async-start(s8[8388608]{0:T(1024)(128)(4,1)} %bitcast.114), calls=%async_computation.1 | async-start | bytes 8388608
  178.1 10.7 %slice-start.2 = ((s8[8388608]{0:T(1024)(128)(4,1)}), s8[4194304]{0:T(1024)(128)(4,1)S(1)}, s32[]{:S(2)}) async-start(s8[8388608]{0:T(1024)(128)(4,1)} %bitcast.118), calls=%async_computation.2 | async-start | bytes 8388608
  178.5 10.2 %slice-start.3 = ((s8[8388608]{0:T(1024)(128)(4,1)}), s8[4194304]{0:T(1024)(128)(4,1)S(1)}, s32[]{:S(2)}) async-start(s8[8388608]{0:T(1024)(128)(4,1)} %bitcast.118), calls=%async_computation.3 | async-start | bytes 8388608
  188.8 7.6 %copy-start.38 = (bf16[592,4096]{1,0:T(8,128)(2,1)S(1)}, bf16[592,4096]{1,0:T(8,128)(2,1)}, u32[]{:S(2)}) copy-start(bf16[592,4096]{1,0:T(8,128)(2,1)} %get-tuple-element.109) | copy-start | bytes 14548996
  236.8 2.3 copy-start.36
  246.0 191.9 %collective-permute-start.2 = (bf16[1,296,1024]{2,1,0:T(8,128)(2,1)}, bf16[1,296,1024]{2,1,0:T(8,128)(2,1)S(1)}, u32[]{:S(2)}, u32[]{:S(2)}) collective-permute-start(bf16[1,296,1024]{2,1,0:T(8,128)(2,1)} %get-tuple-element.91), channel_id=1, source_target_pairs={{0,1},{1,0},{2,3},{3,2},{4,5},{5,4},{6,7},{7,6},{8,9},{9,8},{10,11... | collective-permute-start | bytes 1818632 | tf_op jit(solution)/shard_map/ppermute | solution.py:179
  246.5 27.4 %copy-start.26 = (f32[1024]{0:T(1024)S(1)}, f32[1024]{0:T(1024)}, u32[]{:S(2)}) copy-start(f32[1024]{0:T(1024)} %copy-done.25) | copy-start | bytes 12292
  246.5 27.4 %copy-start.31 = (f32[1024]{0:T(1024)S(1)}, f32[1024]{0:T(1024)}, u32[]{:S(2)}) copy-start(f32[1024]{0:T(1024)} %copy-done.30) | copy-start | bytes 12292
  273.9 9.7 %copy-start.37 = (bf16[1,592,3072]{2,1,0:T(8,128)(2,1)S(1)}, bf16[1,592,3072]{2,1,0:T(8,128)(2,1)}, u32[]{:S(2)}) copy-start(bf16[1,592,3072]{2,1,0:T(8,128)(2,1)} %get-tuple-element.51) | copy-start | bytes 10911748
  292.3 2.6 copy-start.29
  293.3 144.6 %collective-permute-start.3 = (bf16[1,296,1024]{2,1,0:T(8,128)(2,1)}, bf16[1,296,1024]{2,1,0:T(8,128)(2,1)}, u32[]{:S(2)}, u32[]{:S(2)}) collective-permute-start(bf16[1,296,1024]{2,1,0:T(8,128)(2,1)} %get-tuple-element.89), channel_id=1, source_target_pairs={{0,1},{1,0},{2,3},{3,2},{4,5},{5,4},{6,7},{7,6},{8,9},{9,8},{10,11... | collective-permute-start | bytes 1818632 | tf_op jit(solution)/shard_map/ppermute | solution.py:179
  297.2 131.9 %copy-start.24 = (f32[10,32]{1,0:T(8,128)S(1)}, f32[10,32]{1,0:T(8,128)}, u32[]{:S(2)}) copy-start(f32[10,32]{1,0:T(8,128)} %param.27) | copy-start | bytes 3844
  297.2 131.9 %copy-start.27 = (f32[10,32]{1,0:T(8,128)S(1)}, f32[10,32]{1,0:T(8,128)}, u32[]{:S(2)}) copy-start(f32[10,32]{1,0:T(8,128)} %param.33) | copy-start | bytes 3844
  297.2 131.9 %copy-start.28 = (f32[10,32]{1,0:T(8,128)S(1)}, f32[10,32]{1,0:T(8,128)}, u32[]{:S(2)}) copy-start(f32[10,32]{1,0:T(8,128)} %param.39) | copy-start | bytes 3844
  297.2 133.4 %copy-start.8 = (f32[64,1536]{1,0:T(8,128)S(1)}, f32[64,1536]{1,0:T(8,128)}, u32[]{:S(2)}) copy-start(f32[64,1536]{1,0:T(8,128)} %param.22) | copy-start | bytes 1179652
  297.2 133.4 %copy-start.19 = (f32[64,1536]{1,0:T(8,128)S(1)}, f32[64,1536]{1,0:T(8,128)}, u32[]{:S(2)}) copy-start(f32[64,1536]{1,0:T(8,128)} %param.28) | copy-start | bytes 1179652
  297.2 133.4 %copy-start.20 = (f32[64,1536]{1,0:T(8,128)S(1)}, f32[64,1536]{1,0:T(8,128)}, u32[]{:S(2)}) copy-start(f32[64,1536]{1,0:T(8,128)} %param.34) | copy-start | bytes 1179652
  429.0 3.8 copy-start.17
  429.0 3.8 copy-start.18
  429.1 3.8 copy-start.21
  429.1 3.8 copy-start.22
  429.1 4.6 %copy-start.6 = (f32[256,512]{1,0:T(8,128)S(1)}, f32[256,512]{1,0:T(8,128)}, u32[]{:S(2)}) copy-start(f32[256,512]{1,0:T(8,128)} %get-tuple-element.150) | copy-start | bytes 1572868
  429.1 4.6 %copy-start.13 = (f32[256,512]{1,0:T(8,128)S(1)}, f32[256,512]{1,0:T(8,128)}, u32[]{:S(2)}) copy-start(f32[256,512]{1,0:T(8,128)} %param.31) | copy-start | bytes 1572868
  429.1 4.6 %copy-start.14 = (f32[256,512]{1,0:T(8,128)S(1)}, f32[256,512]{1,0:T(8,128)}, u32[]{:S(2)}) copy-start(f32[256,512]{1,0:T(8,128)} %param.37) | copy-start | bytes 1572868
  432.8 2.3 copy-start.33
  432.8 2.3 copy-start.34
  432.8 2.3 copy-start.35
  432.8 3.6 copy-start.5
  432.8 3.6 copy-start.7
  432.8 3.6 copy-start.15
  432.9 3.6 copy-start.16
  436.5 3.1 copy-start.9
  437.9 4.6 %copy-start.12 = (bf16[2,296,1024]{2,1,0:T(8,128)(2,1)}, bf16[2,296,1024]{2,1,0:T(8,128)(2,1)S(1)}, u32[]{:S(2)}) copy-start(bf16[2,296,1024]{2,1,0:T(8,128)(2,1)S(1)} %constant_dynamic-update-slice_fusion.1) | copy-start | bytes 3637252
  439.5 3.1 copy-start.11

commit v3 on v2

--- a/solution.py
+++ b/solution.py
@@ -250,6 +250,9 @@
         mine = out.at[z, x, core, rows, columns(y, width)]
         local = pltpu.make_async_copy(src, mine, own_sem.at[p])
         local.start()
+        if kind == 2:
+            state[p] = [local, push(src, mine, p, depth - 1, site(core, 1 - x, z, y))]
+            return
         state[p] = [local] + [
             push(src, mine, p, k - 1, site(core, x, lax.rem(z + k, depth), y))
             for k in range(1, depth)
@@ -260,6 +263,10 @@
         state[p][0].wait()
         for copy in state[p][1:]:
             copy.wait_recv()
+        if kind == 2:
+            block = out.at[z, :, core, rows, columns(y, width)]
+            state[p] = push(block, block, p, depth, site(core, x, z, 1 - y))
+            return
         block = out.at[:, x, core, rows, columns(y, width)]
         target = site(core, 1 - x, z, y) if kind == 0 else site(core, x, z, 1 - y)
         state[p] = push(block, block, p, depth - 1, target)
@@ -267,6 +274,13 @@
     def stage2(p):
         src, out, rows, width, kind = view(p)
         state[p].wait_recv()
+        if kind == 2:
+            block = out.at[z, :, core, rows, :]
+            state[p] = [
+                push(block, block, p, k - 1, site(core, x, lax.rem(z + k, depth), y))
+                for k in range(1, depth)
+            ]
+            return
         if kind == 0:
             block = out.at[:, :, core, rows, columns(y, width)]
             state[p] = push(block, block, p, depth, site(core, x, z, 1 - y))
@@ -276,30 +290,53 @@
 
     def stage3(p):
         src, out, rows, width, kind = view(p)
-        state[p].wait_recv()
+        for copy in state[p] if kind == 2 else [state[p]]:
+            copy.wait_recv()
         block = out.at[:, :, core, rows, :]
         state[p] = push(block, block, p, depth + 1, site(1 - core, x, z, y))
 
     def stage4(p):
         state[p].wait_recv()
 
-    total = len(parts)
-    for p in range(total):
-        stage0(p)
-    for step in range(total // 2 + 3):
-        for lag, stage in enumerate((stage1, stage2, stage3, stage4)):
-            for p in (2 * (step - lag), 2 * (step - lag) + 1):
-                if 0 <= p < total:
-                    stage(p)
+    in_steps(parts, (stage0, stage1, stage2, stage3, stage4), {1: 0, 2: 1, 3: 99, 4: 99})
     for copy in pending:
         copy.wait_send()
+
+
+def in_steps(parts, stages, when):
+    early = [p for p, part in enumerate(parts) if part[3] == 2]
+    usual = [p for p, part in enumerate(parts) if part[3] != 2]
+    for p in early + usual:
+        stages[0](p)
+    steps = -(-len(usual) // 2) + 3
+    for step in range(steps):
+        for lag, stage in enumerate(stages[1:]):
+            if min(when[lag + 1], steps - 1) == step and when[lag + 1] < 50:
+                for p in early:
+                    stage(p)
+            first = 2 * (step - lag)
+            for p in usual[max(first, 0) : max(first + 2, 0)]:
+                stage(p)
+    for lag, stage in enumerate(stages[1:]):
+        if when[lag + 1] >= 50:
+            for p in early:
+                stage(p)
 
 
 def split_rows(shapes, pieces):
     parts = []
     for w, (shape, n) in enumerate(zip(shapes, pieces)):
-        size = shape[0] // n
-        parts += [(w, i * size, size, i % 2) for i in range(n)]
+        if n:
+            size = shape[0] // n
+            parts += [(w, i * size, size, i % 2) for i in range(n)]
+            continue
+        extra = shape[0] * 3 // 16
+        half = (shape[0] - 2 * extra) // 2
+        big = -(-half // 32) * 16
+        start = 0
+        for size, kind in ((extra, 2), (extra, 2), (big, 0), (big, 1), (half - big, 0), (half - big, 1)):
+            parts.append((w, start, size, kind))
+            start += size
     return parts
 
 
@@ -326,8 +363,8 @@
 def reduce_kernel(parts, depth, count, shapes, *refs):
     grads, outs = refs[:count], refs[count : 2 * count]
     own, near = refs[2 * count : 3 * count], refs[3 * count : 4 * count]
-    mid, side, far, last = (refs[i * count : (i + 1) * count] for i in (4, 5, 6, 7))
-    own_sem, send, recv = refs[8 * count :]
+    mid, side, far, last, ring = (refs[i * count : (i + 1) * count] for i in (4, 5, 6, 7, 8))
+    own_sem, send, recv = refs[9 * count :]
     core, x, z, y = place()
     greet(core, x, z, y, depth)
     pending = []
@@ -381,7 +418,18 @@
             return carry
 
         lax.fori_loop(0, 2 * depth, body, 0)
-        if kind == 0:
+        if kind == 2:
+            state[p] = [
+                push(
+                    own[w].at[lax.rem(z + k, depth), :, rows],
+                    ring[w].at[k - 1, :, rows],
+                    p,
+                    k - 1,
+                    site(core, x, lax.rem(z + k, depth), y),
+                )
+                for k in range(1, depth)
+            ]
+        elif kind == 0:
             state[p] = push(
                 own[w].at[:, :, rows, columns(1 - y, width)],
                 mid[w].at[:, :, rows],
@@ -400,8 +448,27 @@
 
     def stage2(p):
         w, rows, width, kind = view(p)
-        state[p].wait_recv()
-        if kind == 0:
+        for copy in state[p] if kind == 2 else [state[p]]:
+            copy.wait_recv()
+        if kind == 2:
+
+            def body(i, carry):
+                mine = own[w].at[z, i, rows]
+                value = mine[...].astype(jnp.float32)
+                for k in range(depth - 1):
+                    value = value + ring[w][k, i, rows].astype(jnp.float32)
+                mine[...] = value.astype(jnp.bfloat16)
+                return carry
+
+            lax.fori_loop(0, 2, body, 0)
+            state[p] = push(
+                own[w].at[z, :, rows, columns(1 - y, width)],
+                mid[w].at[0, :, rows],
+                p,
+                depth,
+                site(core, x, z, 1 - y),
+            )
+        elif kind == 0:
 
             def body(i, carry):
                 mine = own[w].at[i // 2, lax.rem(i, 2), rows, columns(y, width)]
@@ -435,6 +502,22 @@
     def stage3(p):
         w, rows, width, kind = view(p)
         state[p].wait_recv()
+        if kind == 2:
+
+            def body(i, carry):
+                mine = own[w].at[z, i, rows, columns(y, width)]
+                mine[...] = add(mine, mid[w].at[0, i, rows]).astype(jnp.bfloat16)
+                return carry
+
+            lax.fori_loop(0, 2, body, 0)
+            state[p] = push(
+                own[w].at[z, 1 - x, rows, columns(y, width)],
+                far[w].at[0, rows],
+                p,
+                depth + 1,
+                site(core, 1 - x, z, y),
+            )
+            return
 
         def body(i, carry):
             mine = own[w].at[i, x, rows, columns(y, width)]
@@ -455,6 +538,10 @@
 
     def stage4(p):
         w, rows, width, kind = view(p)
+        if kind == 2:
+            state[p].wait_recv()
+            outs[w][rows] = add(own[w].at[z, x, rows, columns(y, width)], far[w].at[0, rows])
+            return
         for copy in state[p]:
             copy.wait_recv()
         total = own[w][z, x, rows, columns(y, width)].astype(jnp.float32)
@@ -462,14 +549,7 @@
             total = total + last[w][k, rows].astype(jnp.float32)
         outs[w][rows] = total
 
-    total = len(parts)
-    for p in range(total):
-        stage0(p)
-    for step in range(total // 2 + 4):
-        for lag, stage in enumerate((stage1, stage2, stage3, stage4)):
-            for p in (2 * (step - lag), 2 * (step - lag) + 1):
-                if 0 <= p < total:
-                    stage(p)
+    in_steps(parts, (stage0, stage1, stage2, stage3, stage4), {1: 0, 2: 3, 3: 5, 4: 7})
     for copy in pending:
         copy.wait_send()
 
@@ -494,6 +574,10 @@
         + each(lambda r, c: (depth, r, 2 * c))
         + each(lambda r, c: (depth, r, c))
         + each(lambda r, c: (depth - 1, r, c))
+        + [
+            pltpu.VMEM((depth - 1, 2, r, 2 * c) if n == 0 else (8, LANES), jnp.bfloat16)
+            for (r, c), n in zip(shapes, pieces)
+        ]
         + [
             pltpu.SemaphoreType.DMA((total,)),
             pltpu.SemaphoreType.DMA((total, depth + 2)),
@@ -939,7 +1023,7 @@
     each, length = images.shape[:2]
     wide_qkv, wide_small, wide_out, wide_up, wide_down = gather(
         [w_qkv.astype(narrow), small, w_out.astype(narrow), w_up.astype(narrow), w_down.astype(narrow)],
-        (4, 2, 2, 4, 4),
+        (4, 2, 2, 4, 0),
         1,
         depth,
     )
@@ -1009,7 +1093,7 @@
     )
     t_down, t_up, t_out, t_qkv, t_small = reduce_sum(
         [g.astype(narrow) for g in (g_down, g_up, g_outw, g_qkv, g_small)],
-        (4, 4, 2, 4, 2),
+        (0, 4, 2, 4, 2),
         2,
         depth,
     )

time: 446 us -> 436 us (0.978)
  Pallas kernels: 309 us -> 299 us
    pallas_call x1, Pallas kernels: 132 us -> 126 us  [reduce_sum(): pl.pallas_call(functools.partial(reduce_kernel, parts, depth, count, shap...]
    pallas_call x1, Pallas kernels: 132 us -> 128 us  [gather(): pl.pallas_call(functools.partial(gather_kernel, parts, depth, len(shards)...]
  transfers between devices with their start and end apart: 4 -> 4, of which waited for: 0 -> 0; matrix products, arithmetic and copies ran while one was open for 12% -> 12% of each run, Pallas kernels for 70% -> 69%
where the time goes in v3:
time: 436 us; the launch traced here: 432 us
  Pallas kernels  299 us (69%)
  matrix products  94.9 us (22%)
  other arithmetic  19.2 us (4%)
  local copies, waits for them, and re-layouts  13.1 us (3%)
  starting transfers between devices  5.05 us (1%)
    pallas_call x1, Pallas kernels, gather(): pl.pallas_call(functools.partial(gather_kernel, parts, depth, len(shards)...  128 us
    pallas_call x1, Pallas kernels, reduce_sum(): pl.pallas_call(functools.partial(reduce_kernel, parts, depth, count, shap...  126 us
    dot_general x12, matrix products, product(): return lax.dot_general(a, b, dims, preferred_element_type=jnp.float32)  94.9 us
    pallas_call x1, Pallas kernels, attend_back_mixed(): pl.pallas_call(attend_back_mixed_kernel, grid=(count, heads), in_specs=sp...  27.4 us
    pallas_call x1, Pallas kernels, attend_mixed(): pl.pallas_call(attend_mixed_kernel, grid=(count, heads), in_specs=specs +...  16 us
  transfers between devices with their start and end apart: 4, of which 0 were waited for; matrix products, arithmetic and copies ran while one was open for 12% of the time, Pallas kernels for 69%

profile of v3, /device:TPU:0, one launch (start us, length us, event | category | flops | bytes accessed | tf_op | source)
XLA Modules:
  0.0 432.4 jit_solution(13419148319428235497)
XLA Ops:
  0.7 2.3 dynamic-slice_bitcast_fusion
  3.0 3.0 collective-permute-start
  6.0 0.9 constant_dynamic-slice_fusion.1
  6.9 1.7 convert_element_type.110.refs_0_
  8.7 1.5 convert_element_type.111.refs_2_
  10.2 0.7 convert_element_type.112.refs_3_
  10.9 0.7 convert_element_type.113.refs_4_
  11.7 0.6 fusion.45.refs_1_
  12.3 127.7 %shard_map.395 = (bf16[4,2,2,64,3072]{4,3,2,1,0:T(8,128)(2,1)}, bf16[4,2,2,32,256]{4,3,2,1,0:T(8,128)(2,1)}, bf16[4,2,2,64,1024]{4,3,2,1,0:T(8,128)(2,1)}, bf16[...) custom-call(bf16[64,1536]{1,0:T(8,128)(2,1)} %convert_element_type.110.refs_0_, ...), custom_call_target="tpu_custom_call" | custom-call | tf_op jit(solution)/shard_map/pallas_call | solution.py:346
  140.0 1.0 reshape_reshape.6
  141.0 0.1 convert_bitcast_fusion.1
  141.1 0.1 add.259
  141.2 0.1 squeeze.7
  141.3 0.1 squeeze.6
  141.4 0.1 add.253
  141.5 0.1 mul.366
  141.6 0.1 add_compare_fusion.1
  141.6 0.2 copy.53
  141.9 0.1 add.266
  142.0 0.1 add.263
  142.1 0.1 mul.372
  142.2 0.1 add.271
  142.3 0.1 fusion.46
  142.4 0.2 convert_reduce_fusion
  142.6 0.5 fusion.22
  143.1 9.5 %fusion.5.q_ref.k_ref.v_ref = bf16[1,592,3072]{2,1,0:T(8,128)(2,1)} fusion(bf16[1024,3072]{1,0:T(8,128)(2,1)} %bitcast.121, f32[3072]{0:T(1024)S(1)} %pad_maximum_fusion.2, bf16[296,1024]{1,0:T(8,128)(2,1)S(1)} %bitcast.99, bf16[296,1024]{1,0:T(8,128)(2,1)S(1)} %bitcast.94, f32[1024]{0:T(1024)S(1)} %add.253, f32[1024]{0:T(1024)S(1)} %mul.366, ...), kind=kOutput, calls=%fused_computation.12 | convolution fusion | flops 3733635072 | bytes 11166336 | tf_op jit(solution)/shard_map/dot_general | solution.py:1000
  152.6 16.0 %shard_map.396 = (bf16[1,592,1024]{2,1,0:T(8,128)(2,1)S(1)}, f32[1,592,1024]{2,1,0:T(8,128)S(1)}) custom-call(bf16[1,592,3072]{2,1,0:T(8,128)(2,1)} %fusion.5.q_ref.k_ref.v_ref, bf16[1,592,3072]{2,1,0:T(8,128)(2,1)} %fusion.5.q_ref.k_ref.v_ref, bf16[1,592,3072]{2,1,0:T(8,128)(2,1)} %fusion.5.q_ref.k_ref.v_ref, f32[592,1]{1,0:T(8,128)S(1)} %convert_element_type.116.live_ref), custom_call_target="tpu_custom_call" | custom-call | flops 2871001088 | bytes 3637248 | tf_op jit(solution)/shard_map/pallas_call | solution.py:893
  168.7 4.5 %fusion.60 = (f32[592]{0:T(1024)S(1)}, f32[592,1024]{1,0:T(8,128)S(1)}) fusion(f32[1024]{0:T(1024)S(1)} %add.259, bf16[1024,1024]{1,0:T(8,128)(2,1)} %bitcast.123, bf16[1,592,1024]{2,1,0:T(8,128)(2,1)S(1)} %get-tuple-element.44.ctx_ref, bf16[1,296,1024]{2,1,0:T(8,128)(2,1)S(1)} %collective-permute-done.1, bf16[1,296,1024]{2,1,0:T(8,128)(2,1)S(1)} %get-tuple-element.93), kind=kOutput, calls=%fused_computation.120 | convolution fusion | flops 1245756800 | bytes 6953280 | tf_op jit(solution)/shard_map/dot_general | solution.py:1000
  173.2 0.4 multiply_reduce_fusion.2
  173.6 0.3 fusion.28
  173.8 0.2 slice-done.1
  174.0 10.2 %multiply_convert_fusion = (bf16[592,4096]{1,0:T(8,128)(2,1)}, f32[592,4096]{1,0:T(8,128)}) fusion(f32[4096]{0:T(1024)S(1)} %add.266, bf16[1024,4096]{1,0:T(8,128)(2,1)S(1)} %bitcast.116, f32[592,1024]{1,0:T(8,128)S(1)} %get-tuple-element.108, f32[1024]{0:T(1024)S(1)} %add.263, f32[1024]{0:T(1024)S(1)} %mul.372, f32[592]{0:T(1024)S(1)} %add_rsqrt_fusion, ...), kind=kOutput, calls=%fused_computation.6 | convolution fusion | flops 4983635968 | bytes 25391744 | tf_op jit(solution)/shard_map/dot_general | solution.py:1000
  184.3 7.6 %add_convert_fusion.1 = bf16[592,1024]{1,0:T(8,128)(2,1)S(1)} fusion(f32[592,1024]{1,0:T(8,128)S(1)} %get-tuple-element.108, bf16[592,4096]{1,0:T(8,128)(2,1)} %get-tuple-element.109, bf16[4096,1024]{1,0:T(8,128)(2,1)S(1)} %bitcast.120, f32[1024]{0:T(1024)S(1)} %add.271), kind=kOutput, calls=%fused_computation.39 | convolution fusion | flops 4967874560 | bytes 16879616 | tf_op jit(solution)/shard_map/dot_general | solution.py:1000
  191.9 9.1 %convolution_convert_fusion.1 = bf16[4096,1024]{1,0:T(8,128)(2,1)} fusion(bf16[592,4096]{1,0:T(8,128)(2,1)S(1)} %copy-done.38, bf16[592,1024]{1,0:T(8,128)(2,1)S(1)} %fusion.28), kind=kOutput, calls=%fused_computation.9 | convolution fusion | flops 4970250240 | bytes 14450688 | tf_op jit(solution)/shard_map/dot_general | solution.py:1000
  201.0 12.6 %fusion.61 = (f32[4096]{0:T(1024)}, bf16[592,4096]{1,0:T(8,128)(2,1)S(1)}) fusion(f32[592,4096]{1,0:T(8,128)} %get-tuple-element.110, f32[4096]{0:T(1024)S(1)} %add.266, bf16[592,1024]{1,0:T(8,128)(2,1)S(1)} %fusion.28, bf16[4096,1024]{1,0:T(8,128)(2,1)} %bitcast.117), kind=kOutput, calls=%fused_computation.121 | convolution fusion | flops 4995149824 | bytes 24182784 | tf_op jit(solution)/shard_map/dot_general | solution.py:1000
  213.6 9.0 %multiply_reduce_fusion = (f32[1024]{0:T(1024)}, f32[592]{0:T(1024)S(1)}, f32[592]{0:T(1024)S(1)}, f32[1024]{0:T(1024)}, f32[592,1024]{1,0:T(8,128)S(1)}) fusion(f32[592,1024]{1,0:T(8,128)S(1)} %get-tuple-element.108, f32[592]{0:T(1024)S(1)} %add_rsqrt_fusion, f32[592]{0:T(1024)S(1)} %broadcast_multiply_fusion.4, f32[1024]{0:T(1024)S(1)} %mul.372, ...), kind=kOutput, calls=%fused_computation.33 | convolution fusion | flops 4971508736 | bytes 18109696 | tf_op jit(solution)/shard_map/dot_general | solution.py:1000
  222.6 9.7 %convolution_convert_fusion = bf16[1024,4096]{1,0:T(8,128)(2,1)} fusion(bf16[592,4096]{1,0:T(8,128)(2,1)S(1)} %get-tuple-element.114, f32[592,1024]{1,0:T(8,128)S(1)} %get-tuple-element.108, f32[1024]{0:T(1024)S(1)} %add.263, f32[1024]{0:T(1024)S(1)} %mul.372, f32[592]{0:T(1024)S(1)} %add_rsqrt_fusion, f32[592]{0:T(1024)S(1)} %broadcast_multiply_fusion.4), kind=kOutput, calls=%fused_computation.8 | convolution fusion | flops 4973281280 | bytes 15676032 | tf_op jit(solution)/shard_map/dot_general | solution.py:1000
  232.3 2.3 fusion.55
  234.6 2.5 fusion.29.g_ref
  237.1 3.3 convolution_convert_fusion.3
  240.3 0.1 broadcast.196.clone
  240.5 1.0 fusion.57
  241.5 0.5 collective-permute-start.2
  242.0 27.4 %shard_map.397 = (bf16[1,592,3072]{2,1,0:T(8,128)(2,1)}, f32[1,3072]{1,0:T(1,128)}) custom-call(bf16[1,592,3072]{2,1,0:T(8,128)(2,1)} %fusion.5.q_ref.k_ref.v_ref, bf16[1,592,3072]{2,1,0:T(8,128)(2,1)} %fusion.5.q_ref.k_ref.v_ref, bf16[1,592,3072]{2,1,0:T(8,128)(2,1)} %fusion.5.q_ref.k_ref.v_ref, bf16[1,592,1024]{2,1,0:T(8,128)(2,1)} %fusion.29.g_ref, ...), custom_call_target="tpu_custom_call" | custom-call | flops 7177502720 | bytes 7274496 | tf_op jit(solution)/shard_map/pallas_call | solution.py:955
  269.4 9.7 %convolution_convert_fusion.2 = bf16[1024,3072]{1,0:T(8,128)(2,1)} fusion(bf16[1,592,3072]{2,1,0:T(8,128)(2,1)} %get-tuple-element.51, bf16[296,1024]{1,0:T(8,128)(2,1)S(1)} %bitcast.100, bf16[296,1024]{1,0:T(8,128)(2,1)S(1)} %bitcast.95, f32[1024]{0:T(1024)S(1)} %copy-done.31, f32[1024]{0:T(1024)S(1)} %copy-done.26, f32[592]{0:T(1024)S(1)} %add_rsqrt_fusion.1, ...), kind=kOutput, calls=%fused_computation.11 | convolution fusion | flops 3733143552 | bytes 11154048 | tf_op jit(solution)/shard_map/dot_general | solution.py:1000
  279.1 7.3 %fusion.21 = (f32[1024]{0:T(1024)}, f32[592]{0:T(1024)S(1)}, f32[592]{0:T(1024)S(1)}, f32[1024]{0:T(1024)}, f32[592,1024]{1,0:T(8,128)S(1)}) fusion(f32[592]{0:T(1024)S(1)} %add_rsqrt_fusion.1, f32[592]{0:T(1024)S(1)} %broadcast_multiply_fusion.5, bf16[1,296,1024]{2,1,0:T(8,128)(2,1)S(1)} %collective-permute-done.1, ...), kind=kOutput, calls=%fused_computation.30 | convolution fusion | flops 3732419584 | bytes 13587712 | tf_op jit(solution)/shard_map/dot_general | solution.py:1000
  286.4 1.4 fusion.30
  287.8 0.1 broadcast.196.clone.1
  287.9 0.9 fusion.56
  288.8 1.5 collective-permute-start.3
  290.4 0.6 fusion.59
  291.0 1.7 shard_map.398
  292.7 125.8 %shard_map.399 = (f32[256,512]{1,0:T(8,128)}, f32[64,2048]{1,0:T(8,128)}, f32[64,512]{1,0:T(8,128)}, f32[64,1536]{1,0:T(8,128)}, f32[32,128]{1,0:T(8,128)}) custom-call(bf16[4,2,2,256,1024]{4,3,2,1,0:T(8,128)(2,1)} %bitcast.96, bf16[4,2,2,64,4096]{4,3,2,1,0:T(8,128)(2,1)} %bitcast.97, bf16[4,2,2,64,1024]{4,3,2,1,0:T(8,128)(2,1)} %bitcast.103, ...), custom_call_target="tpu_custom_call" | custom-call | tf_op jit(solution)/shard_map/pallas_call | solution.py:566
  418.7 1.5 multiply_subtract_fusion.4
  420.2 2.2 multiply_subtract_fusion.2
  422.5 0.8 multiply_subtract_fusion.3
  423.3 1.4 multiply_subtract_fusion
  424.7 1.3 multiply_subtract_fusion.5
  426.0 1.4 multiply_subtract_fusion.1
  427.5 1.5 constant_dynamic-update-slice_fusion
  429.1 0.8 copy.64
  429.9 0.7 copy.65
  430.5 0.8 copy.66
  431.3 0.8 copy.67
  (111 shorter events, 0.4 us)
Async XLA Ops:
  0.7 5.3 %copy-start.10 = (bf16[2,296,1024]{2,1,0:T(8,128)(2,1)S(1)}, bf16[2,296,1024]{2,1,0:T(8,128)(2,1)}, u32[]{:S(2)}) copy-start(bf16[2,296,1024]{2,1,0:T(8,128)(2,1)} %param.20) | copy-start | bytes 3637252
  0.7 7.9 %copy-start.23 = (f32[10,32]{1,0:T(8,128)S(1)}, f32[10,32]{1,0:T(8,128)}, u32[]{:S(2)}) copy-start(f32[10,32]{1,0:T(8,128)} %param.27) | copy-start | bytes 3844
  0.7 7.9 %copy-start.32 = (f32[2,32]{1,0:T(2,128)S(1)}, f32[2,32]{1,0:T(2,128)}, u32[]{:S(2)}) copy-start(f32[2,32]{1,0:T(2,128)} %param.26) | copy-start | bytes 772
  0.7 9.5 %copy-start.4 = (f32[64,2048]{1,0:T(8,128)S(1)}, f32[64,2048]{1,0:T(8,128)}, u32[]{:S(2)}) copy-start(f32[64,2048]{1,0:T(8,128)} %param.24) | copy-start | bytes 1572868
  3.0 7.9 %copy-start.3 = (f32[256,512]{1,0:T(8,128)S(1)}, f32[256,512]{1,0:T(8,128)}, u32[]{:S(2)}) copy-start(f32[256,512]{1,0:T(8,128)} %param.25) | copy-start | bytes 1572868
  3.0 170.5 %collective-permute-start = (bf16[1,296,1024]{2,1,0:T(8,128)(2,1)}, bf16[1,296,1024]{2,1,0:T(8,128)(2,1)S(1)}, u32[]{:S(2)}, u32[]{:S(2)}) collective-permute-start(bf16[1,296,1024]{2,1,0:T(8,128)(2,1)} %get-tuple-element.96), channel_id=1, source_target_pairs={{0,1},{1,0},{2,3},{3,2},{4,5},{5,4},{6,7},{7,6},{8,9},{9,8},{10,11... | collective-permute-start | bytes 1818632 | tf_op jit(solution)/shard_map/ppermute | solution.py:166
  6.9 135.4 %collective-permute-start.1 = (bf16[1,296,1024]{2,1,0:T(8,128)(2,1)}, bf16[1,296,1024]{2,1,0:T(8,128)(2,1)S(1)}, u32[]{:S(2)}, u32[]{:S(2)}) collective-permute-start(bf16[1,296,1024]{2,1,0:T(8,128)(2,1)} %get-tuple-element.94), channel_id=1, source_target_pairs={{0,1},{1,0},{2,3},{3,2},{4,5},{5,4},{6,7},{7,6},{8,9},{9,8},{10,11... | collective-permute-start | bytes 1818632 | tf_op jit(solution)/shard_map/ppermute | solution.py:166
  141.5 11.2 %copy-start.30 = (f32[1024]{0:T(1024)}, f32[1024]{0:T(1024)S(1)}, u32[]{:S(2)}) copy-start(f32[1024]{0:T(1024)S(1)} %add.253) | copy-start | bytes 12292
  141.5 11.1 %copy-start.25 = (f32[1024]{0:T(1024)}, f32[1024]{0:T(1024)S(1)}, u32[]{:S(2)}) copy-start(f32[1024]{0:T(1024)S(1)} %mul.366) | copy-start | bytes 12292
  141.9 10.7 %copy-start = (f32[592,1]{1,0:T(8,128)}, f32[592,1]{1,0:T(8,128)S(1)}, u32[]{:S(2)}) copy-start(f32[592,1]{1,0:T(8,128)S(1)} %convert_element_type.116.live_ref) | copy-start | bytes 7108
  168.6 4.5 %copy-start.1 = (f32[1,592,1024]{2,1,0:T(8,128)}, f32[1,592,1024]{2,1,0:T(8,128)S(1)}, u32[]{:S(2)}) copy-start(f32[1,592,1024]{2,1,0:T(8,128)S(1)} %get-tuple-element.50.lse_ref) | copy-start | bytes 7274500
  168.6 68.4 %copy-start.2 = (bf16[1,592,1024]{2,1,0:T(8,128)(2,1)}, bf16[1,592,1024]{2,1,0:T(8,128)(2,1)S(1)}, u32[]{:S(2)}) copy-start(bf16[1,592,1024]{2,1,0:T(8,128)(2,1)S(1)} %get-tuple-element.44.ctx_ref) | copy-start | bytes 3637252
  168.6 5.2 %slice-start = ((s8[8388608]{0:T(1024)(128)(4,1)}), s8[4194304]{0:T(1024)(128)(4,1)S(1)}, s32[]{:S(2)}) async-start(s8[8388608]{0:T(1024)(128)(4,1)} %bitcast.114), calls=%async_computation | async-start | bytes 8388608
  168.7 5.4 %slice-start.1 = ((s8[8388608]{0:T(1024)(128)(4,1)}), s8[4194304]{0:T(1024)(128)(4,1)S(1)}, s32[]{:S(2)}) async-start(s8[8388608]{0:T(1024)(128)(4,1)} %bitcast.114), calls=%async_computation.1 | async-start | bytes 8388608
  173.6 10.7 %slice-start.2 = ((s8[8388608]{0:T(1024)(128)(4,1)}), s8[4194304]{0:T(1024)(128)(4,1)S(1)}, s32[]{:S(2)}) async-start(s8[8388608]{0:T(1024)(128)(4,1)} %bitcast.118), calls=%async_computation.2 | async-start | bytes 8388608
  174.0 10.2 %slice-start.3 = ((s8[8388608]{0:T(1024)(128)(4,1)}), s8[4194304]{0:T(1024)(128)(4,1)S(1)}, s32[]{:S(2)}) async-start(s8[8388608]{0:T(1024)(128)(4,1)} %bitcast.118), calls=%async_computation.3 | async-start | bytes 8388608
  184.3 7.6 %copy-start.38 = (bf16[592,4096]{1,0:T(8,128)(2,1)S(1)}, bf16[592,4096]{1,0:T(8,128)(2,1)}, u32[]{:S(2)}) copy-start(bf16[592,4096]{1,0:T(8,128)(2,1)} %get-tuple-element.109) | copy-start | bytes 14548996
  232.3 2.3 copy-start.36
  241.5 186.0 %collective-permute-start.2 = (bf16[1,296,1024]{2,1,0:T(8,128)(2,1)}, bf16[1,296,1024]{2,1,0:T(8,128)(2,1)S(1)}, u32[]{:S(2)}, u32[]{:S(2)}) collective-permute-start(bf16[1,296,1024]{2,1,0:T(8,128)(2,1)} %get-tuple-element.91), channel_id=1, source_target_pairs={{0,1},{1,0},{2,3},{3,2},{4,5},{5,4},{6,7},{7,6},{8,9},{9,8},{10,11... | collective-permute-start | bytes 1818632 | tf_op jit(solution)/shard_map/ppermute | solution.py:179
  242.0 27.4 %copy-start.26 = (f32[1024]{0:T(1024)S(1)}, f32[1024]{0:T(1024)}, u32[]{:S(2)}) copy-start(f32[1024]{0:T(1024)} %copy-done.25) | copy-start | bytes 12292
  242.0 27.4 %copy-start.31 = (f32[1024]{0:T(1024)S(1)}, f32[1024]{0:T(1024)}, u32[]{:S(2)}) copy-start(f32[1024]{0:T(1024)} %copy-done.30) | copy-start | bytes 12292
  269.4 9.7 %copy-start.37 = (bf16[1,592,3072]{2,1,0:T(8,128)(2,1)S(1)}, bf16[1,592,3072]{2,1,0:T(8,128)(2,1)}, u32[]{:S(2)}) copy-start(bf16[1,592,3072]{2,1,0:T(8,128)(2,1)} %get-tuple-element.51) | copy-start | bytes 10911748
  287.8 2.6 copy-start.29
  288.8 138.7 %collective-permute-start.3 = (bf16[1,296,1024]{2,1,0:T(8,128)(2,1)}, bf16[1,296,1024]{2,1,0:T(8,128)(2,1)}, u32[]{:S(2)}, u32[]{:S(2)}) collective-permute-start(bf16[1,296,1024]{2,1,0:T(8,128)(2,1)} %get-tuple-element.89), channel_id=1, source_target_pairs={{0,1},{1,0},{2,3},{3,2},{4,5},{5,4},{6,7},{7,6},{8,9},{9,8},{10,11... | collective-permute-start | bytes 1818632 | tf_op jit(solution)/shard_map/ppermute | solution.py:179
  292.7 126.0 %copy-start.24 = (f32[10,32]{1,0:T(8,128)S(1)}, f32[10,32]{1,0:T(8,128)}, u32[]{:S(2)}) copy-start(f32[10,32]{1,0:T(8,128)} %param.27) | copy-start | bytes 3844
  292.7 126.0 %copy-start.27 = (f32[10,32]{1,0:T(8,128)S(1)}, f32[10,32]{1,0:T(8,128)}, u32[]{:S(2)}) copy-start(f32[10,32]{1,0:T(8,128)} %param.33) | copy-start | bytes 3844
  292.7 126.0 %copy-start.28 = (f32[10,32]{1,0:T(8,128)S(1)}, f32[10,32]{1,0:T(8,128)}, u32[]{:S(2)}) copy-start(f32[10,32]{1,0:T(8,128)} %param.39) | copy-start | bytes 3844
  292.7 127.5 %copy-start.8 = (f32[64,1536]{1,0:T(8,128)S(1)}, f32[64,1536]{1,0:T(8,128)}, u32[]{:S(2)}) copy-start(f32[64,1536]{1,0:T(8,128)} %param.22) | copy-start | bytes 1179652
  292.7 127.5 %copy-start.19 = (f32[64,1536]{1,0:T(8,128)S(1)}, f32[64,1536]{1,0:T(8,128)}, u32[]{:S(2)}) copy-start(f32[64,1536]{1,0:T(8,128)} %param.28) | copy-start | bytes 1179652
  292.7 127.5 %copy-start.20 = (f32[64,1536]{1,0:T(8,128)S(1)}, f32[64,1536]{1,0:T(8,128)}, u32[]{:S(2)}) copy-start(f32[64,1536]{1,0:T(8,128)} %param.34) | copy-start | bytes 1179652
  418.6 3.8 copy-start.17
  418.6 3.8 copy-start.18
  418.6 3.8 copy-start.21
  418.6 3.8 copy-start.22
  418.6 4.6 %copy-start.6 = (f32[256,512]{1,0:T(8,128)S(1)}, f32[256,512]{1,0:T(8,128)}, u32[]{:S(2)}) copy-start(f32[256,512]{1,0:T(8,128)} %get-tuple-element.150) | copy-start | bytes 1572868
  418.6 4.6 %copy-start.13 = (f32[256,512]{1,0:T(8,128)S(1)}, f32[256,512]{1,0:T(8,128)}, u32[]{:S(2)}) copy-start(f32[256,512]{1,0:T(8,128)} %param.31) | copy-start | bytes 1572868
  418.7 4.6 %copy-start.14 = (f32[256,512]{1,0:T(8,128)S(1)}, f32[256,512]{1,0:T(8,128)}, u32[]{:S(2)}) copy-start(f32[256,512]{1,0:T(8,128)} %param.37) | copy-start | bytes 1572868
  422.4 2.3 copy-start.33
  422.4 2.3 copy-start.34
  422.4 2.3 copy-start.35
  422.4 3.6 copy-start.5
  422.4 3.6 copy-start.7
  422.4 3.6 copy-start.15
  422.4 3.6 copy-start.16
  426.0 3.1 copy-start.9
  427.5 4.6 %copy-start.12 = (bf16[2,296,1024]{2,1,0:T(8,128)(2,1)}, bf16[2,296,1024]{2,1,0:T(8,128)(2,1)S(1)}, u32[]{:S(2)}) copy-start(bf16[2,296,1024]{2,1,0:T(8,128)(2,1)S(1)} %constant_dynamic-update-slice_fusion.1) | copy-start | bytes 3637252
  429.1 3.1 copy-start.11
